TPU v7x, 1024 devices: a whole 4x8x16 slice. The times are simulated.
1024 devices in a mesh: ctx: 64 (over x, z), head: 16 (over y, core).
Axes of the slice: x: 4, y: 8, z: 16, core: 2. Of those that a mesh axis runs over, the one named last changes fastest.
Arguments:
- tokens: float32 [32768, 2048], P('ctx', 'head'), may hold values from -6 to 6
- w_proj: float32 [2048, 8192], P(None, 'head'), may hold values from -0.125 to 0.125
- w_mix: float32 [2048, 144], P(None, 'head'), may hold values from -0.125 to 0.125
- conv_w: float32 [4, 6144], P(None, 'head'), may hold values from -3 to 3
- rates: float32 [16], P('head'), may hold values from 0.0001 to 0.05
- doc_start: int32 [32768], P('ctx'), may hold values 0 or 1
- norm_gain: float32 [2048], P('head'), may hold values from 0.5 to 1.5
- w_out: float32 [2048, 2048], P(None, 'head'), may hold values from -0.125 to 0.125
Outputs:
- output: float32 [32768, 2048], P('ctx', 'head')
All inputs are finite; a program needn't handle non-finite values. No bound on the sum of `doc_start` on one device may be relied on, other than what follows from the above.
Results may differ from a plain program's by a relative error of at most 0.00021.
Values sent between devices are 32-bit elements; how exact they have to be, the bound alone decides.
A program may use at most 32 MiB of HBM per device.

v0:
```python
import jax
import jax.numpy as jnp
from jax import lax
from jax.sharding import PartitionSpec as P


def shifted(value, axis, steps):
    count = lax.axis_size(axis)
    initial, last = (max(0, -steps), min(count, count - steps))
    return lax.ppermute(value, axis, [(source, source + steps) for source in range(initial, last)])


def partner(value, axis, bit):
    mask = 2**bit
    pairs = [(source, source ^ mask) for source in range(lax.axis_size(axis))]
    return lax.ppermute(value, axis, pairs)


def shards(tokens, w_proj, w_mix, conv_w, rates, doc_start, norm_gain, w_out):
    highest = lax.Precision.HIGHEST
    tok_rows = tokens.shape[0]
    width = w_proj.shape[1] // 4
    kernel = conv_w.shape[0]
    rim_rows = kernel - 1
    portion = lax.all_gather(tokens, "head", axis=1, tiled=True)
    projected = jnp.dot(portion, w_proj, precision=highest, preferred_element_type=jnp.float32)
    mixing = jnp.dot(portion, w_mix, precision=highest, preferred_element_type=jnp.float32)
    raw_qkv = projected[:, : 3 * width]
    prior_qkv = shifted(raw_qkv[tok_rows - rim_rows :], "ctx", 1)
    padded = jnp.concatenate([prior_qkv, raw_qkv], axis=0)
    gate_raw = projected[:, 3 * width :]
    convolved = jnp.zeros((tok_rows, 3 * width), jnp.float32)
    for step in range(kernel):
        convolved = convolved + conv_w[step][None, :] * padded[step : step + tok_rows]
    convolved = jax.nn.silu(convolved)
    query = convolved[:, :width]
    keys = convolved[:, width : 2 * width]
    values = convolved[:, 2 * width :]
    query = query / jnp.sqrt(jnp.sum(query * query, axis=1, keepdims=True) + 1e-06)
    keys = keys / jnp.sqrt(jnp.sum(keys * keys, axis=1, keepdims=True) + 1e-06)
    beta = jax.nn.sigmoid(mixing[:, 0])
    log_decay = -rates[0] * jax.nn.softplus(mixing[:, 1]) - 20.0 * doc_start.astype(jnp.float32)
    weights = jax.nn.softplus(mixing[:, 2:])
    cumlog = jnp.cumsum(log_decay)
    row_ids = jnp.arange(tok_rows)[:, None]
    col_ids = jnp.arange(tok_rows)[None, :]
    lower_incl = row_ids >= col_ids
    strict_lower = row_ids > col_ids
    decay_grid = jnp.exp(jnp.where(lower_incl, cumlog[:, None] - cumlog[None, :], -jnp.inf))
    key_gram = jnp.dot(keys, keys.T, precision=highest, preferred_element_type=jnp.float32)
    identity_t = jnp.eye(tok_rows, dtype=jnp.float32)
    identity_d = jnp.eye(width, dtype=jnp.float32)
    lhs_plain = identity_t + beta[:, None] * jnp.where(strict_lower, key_gram, 0.0)
    factor_x = jax.scipy.linalg.solve_triangular(
        lhs_plain, beta[:, None] * keys, lower=True, unit_diagonal=True
    )
    lhs_decay = identity_t + beta[:, None] * jnp.where(strict_lower, decay_grid * key_gram, 0.0)
    factor_y = jax.scipy.linalg.solve_triangular(
        lhs_decay, beta[:, None] * values, lower=True, unit_diagonal=True
    )
    gamma = jnp.exp(cumlog)
    block_a = gamma[-1] * (
        identity_d
        - jnp.dot(factor_x.T, keys, precision=highest, preferred_element_type=jnp.float32)
    )
    tail = jnp.exp(cumlog[-1] - cumlog)
    block_b = jnp.dot(
        (factor_y * tail[:, None]).T, keys, precision=highest, preferred_element_type=jnp.float32
    )
    qk_grid = jnp.dot(query, keys.T, precision=highest, preferred_element_type=jnp.float32)
    carried = gamma[:, None] * (
        query
        - jnp.dot(
            jnp.where(lower_incl, qk_grid, 0.0),
            factor_x,
            precision=highest,
            preferred_element_type=jnp.float32,
        )
    )
    local = jnp.dot(
        decay_grid * qk_grid, factor_y, precision=highest, preferred_element_type=jnp.float32
    )
    my_index = lax.axis_index("ctx")
    nbits = lax.axis_size("ctx").bit_length() - 1
    group_a, group_b = (block_a, block_b)
    carry_m = identity_d
    level_states = []
    for level in range(nbits):
        other_a, other_b = partner((group_a, group_b), "ctx", level)
        upper = my_index >> level & 1 == 1
        seg_a = jnp.where(upper, other_a, identity_d)
        seg_b = jnp.where(upper, other_b, 0.0)
        first_a = jnp.where(upper, other_a, group_a)
        first_b = jnp.where(upper, other_b, group_b)
        second_a = jnp.where(upper, group_a, other_a)
        second_b = jnp.where(upper, group_b, other_b)
        group_a = jnp.dot(first_a, second_a, precision=highest, preferred_element_type=jnp.float32)
        group_b = (
            jnp.dot(first_b, second_a, precision=highest, preferred_element_type=jnp.float32)
            + second_b
        )
        level_states.append(
            jnp.dot(seg_b, carry_m, precision=highest, preferred_element_type=jnp.float32)
        )
        carry_m = jnp.dot(seg_a, carry_m, precision=highest, preferred_element_type=jnp.float32)
    mixed = weights[:, 0:1] * local
    for level in range(nbits):
        mixed = mixed + weights[:, level + 1 : level + 2] * jnp.dot(
            carried, level_states[level].T, precision=highest, preferred_element_type=jnp.float32
        )
    scale = jnp.sqrt(jnp.mean(mixed * mixed, axis=1, keepdims=True) + 1e-05)
    normed = mixed / scale * norm_gain[None, :] * jax.nn.silu(gate_raw)
    own_rows = lax.all_to_all(w_out, "head", split_axis=0, concat_axis=1, tiled=True)
    partial_out = jnp.dot(normed, own_rows, precision=highest, preferred_element_type=jnp.float32)
    result = lax.psum_scatter(partial_out, "head", scatter_dimension=1, tiled=True)
    return result


def solution(mesh):
    placed = (
        P("ctx", "head"),
        P(None, "head"),
        P(None, "head"),
        P(None, "head"),
        P("head"),
        P("ctx"),
        P("head"),
        P(None, "head"),
    )
    return jax.shard_map(
        shards, mesh=mesh, in_specs=placed, out_specs=P("ctx", "head"), check_vma=False
    )
```

profile of v0, /device:TPU:1, one launch (start us, length us, event | category | flops | bytes accessed | tf_op | source)
XLA Modules:
  0.0 399.0 jit_solution(10839584713523618747)
XLA Ops:
  7.3 17.6 %all-to-all-start = ((f32[16,128,128]{2,1,0:T(8,128)}), f32[16,128,128]{2,1,0:T(8,128)S(1)}, u32[]{:S(2)}, u32[]{:S(2)}) async-start(f32[16,128,128]{2,1,0:T(8,128)} %bitcast.100), calls=%async_computation | async-start | bytes 2097152 | tf_op jit(solution)/shard_map/all_to_all | solution.py:113
  27.6 28.1 %all-to-all-done = f32[16,128,128]{2,1,0:T(8,128)S(1)} async-done(((f32[16,128,128]{2,1,0:T(8,128)}), f32[16,128,128]{2,1,0:T(8,128)S(1)}, u32[]{:S(2)}, u32[]{:S(2)}) %all-to-all-start) | async-done | bytes 1048608 | tf_op jit(solution)/shard_map/all_to_all | solution.py:113
  56.0 29.6 %all-gather.2.cloned.1.call-done = f32[512,2048]{1,0:T(8,128)} async-done(((f32[512,128]{1,0:T(8,128)}), f32[512,2048]{1,0:T(8,128)}) %all-gather.2.cloned.1.call-update) | async-done | bytes 4194320 | tf_op jit(solution)/shard_map/all_gather | solution.py:25
  85.6 5.9 %fusion.157 = f32[512,9]{0,1:T(8,128)S(1)} fusion(f32[512,2048]{1,0:T(8,128)} %all-gather.2.cloned.1.call-done, f32[2048,9]{0,1:T(8,128)S(1)} %copy-done), kind=kOutput, calls=%fused_computation.237 | convolution fusion | flops 113246208 | bytes 4286464 | tf_op jit(solution)/shard_map/dot_general | solution.py:27
  92.2 9.0 %fusion.158 = f32[512,512]{1,0:T(8,128)S(1)} fusion(f32[512,2048]{1,0:T(8,128)S(1)} %copy-done.1, f32[2048,512]{1,0:T(8,128)} %param.11), kind=kOutput, calls=%fused_computation.238 | convolution fusion | flops 6442450944 | bytes 9437184 | tf_op jit(solution)/shard_map/dot_general | solution.py:26
  108.6 3.3 convert_add_fusion
  112.7 14.0 %while.5 = (s32[]{:T(128)}, f32[512,512]{1,0:T(8,128)}, s32[4,2]{0,1:T(2,128)S(1)}, f32[4,128,128]{2,1,0:T(8,128)}, s32[]{:T(128)}) while((s32[]{:T(128)}, f32[512,512]{1,0:T(8,128)}, s32[4,2]{0,1:T(2,128)S(1)}, f32[4,128,128]{2,1,0:T(8,128)}, s32[]{:T(128)}) %tuple.53), condition=%wide.while_cond.clone, body=%wide.while_body.clone.sunk | while | flops 2 | bytes 132705 | solution.py:54
  113.3 2.9 bitcast_dynamic-update-slice_fusion.5
  116.8 2.9 bitcast_dynamic-update-slice_fusion.5
  120.4 2.9 bitcast_dynamic-update-slice_fusion.5
  123.9 2.8 bitcast_dynamic-update-slice_fusion.5
  126.7 40.7 %custom-call.5 = f32[4,128,128]{1,2,0:T(8,128)} custom-call(f32[4,128,128]{2,1,0:T(8,128)} %get-tuple-element.21), custom_call_target="InvertDiagBlocksLowerTriangular" | custom-call | tf_op jit(solution)/shard_map/jit(_solve_triangular)/triangular_solve | solution.py:54
  176.2 2.0 fusion.7
  178.2 2.1 collective-permute-start.2
  181.0 13.8 %while.4 = (s32[]{:T(128)}, f32[512,512]{1,0:T(8,128)}, s32[4,2]{0,1:T(2,128)S(1)}, f32[4,128,128]{2,1,0:T(8,128)}, s32[]{:T(128)}) while((s32[]{:T(128)}, f32[512,512]{1,0:T(8,128)}, s32[4,2]{0,1:T(2,128)S(1)}, f32[4,128,128]{2,1,0:T(8,128)}, s32[]{:T(128)}) %tuple.60), condition=%wide.while_cond, body=%wide.while_body.sunk | while | flops 2 | bytes 132705 | solution.py:58
  181.6 2.8 bitcast_dynamic-update-slice_fusion.4
  185.1 2.8 bitcast_dynamic-update-slice_fusion.4
  188.5 2.8 bitcast_dynamic-update-slice_fusion.4
  192.0 2.8 bitcast_dynamic-update-slice_fusion.4
  194.7 40.7 %custom-call.4 = f32[4,128,128]{1,2,0:T(8,128)} custom-call(f32[4,128,128]{2,1,0:T(8,128)} %get-tuple-element.20), custom_call_target="InvertDiagBlocksLowerTriangular" | custom-call | tf_op jit(solution)/shard_map/jit(_solve_triangular)/triangular_solve | solution.py:58
  245.0 3.6 collective-permute-start.1
  254.8 1.9 collective-permute-start.4
  256.9 4.3 %collective-permute-start.3 = (f32[128,128]{1,0:T(8,128)S(1)}, f32[128,128]{1,0:T(8,128)S(1)}, u32[]{:S(2)}, u32[]{:S(2)}) collective-permute-start(f32[128,128]{1,0:T(8,128)S(1)} %convolution_add_fusion.4), channel_id=1, source_target_pairs={{0,32},{16,48},{32,0},{48,16},{64,96},{80,112},{96,64},{112,80},{1... | collective-permute-start | bytes 196616 | tf_op jit(solution)/shard_map/ppermute | solution.py:16
  262.8 8.7 %collective-permute-start.6 = (f32[128,128]{1,0:T(8,128)S(1)}, f32[128,128]{1,0:T(8,128)S(1)}, u32[]{:S(2)}, u32[]{:S(2)}) collective-permute-start(f32[128,128]{1,0:T(8,128)S(1)} %fusion.90), channel_id=1, source_target_pairs={{0,64},{16,80},{32,96},{48,112},{64,0},{80,16},{96,32},{112,48},{1... | collective-permute-start | bytes 196616 | tf_op jit(solution)/shard_map/ppermute | solution.py:16
  271.7 3.0 collective-permute-start.5
  275.7 10.3 %collective-permute-start.8 = (f32[128,128]{1,0:T(8,128)S(1)}, f32[128,128]{1,0:T(8,128)S(1)}, u32[]{:S(2)}, u32[]{:S(2)}) collective-permute-start(f32[128,128]{1,0:T(8,128)S(1)} %fusion.85), channel_id=1, source_target_pairs={{0,128},{16,144},{32,160},{48,176},{64,192},{80,208},{96,224},{112... | collective-permute-start | bytes 196616 | tf_op jit(solution)/shard_map/ppermute | solution.py:16
  286.2 8.7 %collective-permute-start.7 = (f32[128,128]{1,0:T(8,128)S(1)}, f32[128,128]{1,0:T(8,128)S(1)}, u32[]{:S(2)}, u32[]{:S(2)}) collective-permute-start(f32[128,128]{1,0:T(8,128)S(1)} %convolution_add_fusion.2), channel_id=1, source_target_pairs={{0,128},{16,144},{32,160},{48,176},{64,192},{80,208},{96,224},{112... | collective-permute-start | bytes 196616 | tf_op jit(solution)/shard_map/ppermute | solution.py:16
  296.0 3.1 collective-permute-start.10
  300.2 3.1 collective-permute-start.9
  305.5 4.7 %collective-permute-start.11 = (f32[128,128]{1,0:T(8,128)S(1)}, f32[128,128]{1,0:T(8,128)S(1)}, u32[]{:S(2)}, u32[]{:S(2)}) collective-permute-start(f32[128,128]{1,0:T(8,128)S(1)} %convolution_add_fusion), channel_id=1, source_target_pairs={{0,512},{16,528},{32,544},{48,560},{64,576},{80,592},{96,608},{112... | collective-permute-start | bytes 196616 | tf_op jit(solution)/shard_map/ppermute | solution.py:16
  312.7 5.1 %fusion.24 = f32[512,2048]{1,0:T(8,128)} fusion(f32[128,2048]{0,1:T(8,128)S(1)} %bitcast.99, f32[512,512]{1,0:T(8,128)S(1)} %fusion.158, f32[512,128]{1,0:T(8,128)S(1)} %get-tuple-element.64, f32[128]{0:T(128)S(1)} %copy-done.17, f32[512]{0:T(512)S(1)} %add_sqrt_fusion), kind=kOutput, calls=%fused_computation.65 | convolution fusion | flops 1611071488 | bytes 5769728 | tf_op jit(solution)/shard_map/dot_general | solution.py:114
  317.8 74.3 %reduce-scatter.2.cloned.1.call-done = f32[512,128]{1,0:T(8,128)} async-done(((f32[512,2048]{1,0:T(8,128)}), f32[512,128]{1,0:T(8,128)}) %reduce-scatter.2.cloned.1.call-update) | async-done | bytes 262160 | tf_op jit(solution)/shard_map/reduce_scatter | solution.py:115
  (142 shorter events, 51.6 us)
Async XLA Ops:
  6.5 79.1 %copy-start = (f32[2048,9]{0,1:T(8,128)S(1)}, f32[2048,9]{0,1:T(8,128)}, u32[]{:S(2)}) copy-start(f32[2048,9]{0,1:T(8,128)} %param.12) | copy-start | bytes 221188
  6.5 79.1 %all-gather.2.cloned.1.call-start = ((), (), s32[]{:S(2)}) async-start(), calls=%async_computation.2 | async-start | bytes 4456448 | tf_op jit(solution)/shard_map/all_gather | solution.py:25
  7.3 48.4 %all-to-all-start = ((f32[16,128,128]{2,1,0:T(8,128)}), f32[16,128,128]{2,1,0:T(8,128)S(1)}, u32[]{:S(2)}, u32[]{:S(2)}) async-start(f32[16,128,128]{2,1,0:T(8,128)} %bitcast.100), calls=%async_computation | async-start | bytes 2097152 | tf_op jit(solution)/shard_map/all_to_all | solution.py:113
  24.9 367.2 %reduce-scatter.2.cloned.1.call-start = ((), (), s32[]{:S(2)}) async-start(), calls=%async_computation.3 | async-start | bytes 4456448 | tf_op jit(solution)/shard_map/reduce_scatter | solution.py:115
  85.6 6.5 %copy-start.1 = (f32[512,2048]{1,0:T(8,128)S(1)}, f32[512,2048]{1,0:T(8,128)}, u32[]{:S(2)}) copy-start(f32[512,2048]{1,0:T(8,128)} %all-gather.2.cloned.1.call-done) | copy-start | bytes 12582916
  92.2 10.5 %copy-start.15 = (s32[512]{0:T(512)S(1)}, s32[512]{0:T(512)}, u32[]{:S(2)}) copy-start(s32[512]{0:T(512)} %param.15) | copy-start | bytes 6148
  101.3 5.1 %collective-permute-start = (f32[3,384]{1,0:T(4,128)S(1)}, f32[3,384]{1,0:T(4,128)S(1)}, u32[]{:S(2)}, u32[]{:S(2)}) collective-permute-start(f32[3,384]{1,0:T(4,128)S(1)} %slice.148), channel_id=1, source_target_pairs={{0,16},{16,32},{32,48},{48,64},{64,80},{80,96},{96,112},{112,128},... | collective-permute-start | bytes 13832 | tf_op jit(solution)/shard_map/ppermute | solution.py:10
  103.4 4.3 %copy-start.16 = (f32[512]{0:T(512)}, f32[512]{0:T(512)S(1)}, u32[]{:S(2)}) copy-start(f32[512]{0:T(512)S(1)} %get-tuple-element.44) | copy-start | bytes 6148
  103.4 8.5 %copy-start.14 = (f32[512]{0:T(512)}, f32[512]{0:T(512)S(1)}, u32[]{:S(2)}) copy-start(f32[512]{0:T(512)S(1)} %get-tuple-element.45) | copy-start | bytes 6148
  106.9 5.1 %copy-start.18 = (s32[4]{0:T(128)S(1)}, s32[4]{0:T(128)}, u32[]{:S(2)}) copy-start(s32[4]{0:T(128)} %iota_multiply_fusion) | copy-start | bytes 52
  168.6 7.0 %copy-start.2 = (f32[128,128]{1,0:T(8,128)}, f32[128,128]{1,0:T(8,128)S(1)}, u32[]{:S(2)}) copy-start(f32[128,128]{1,0:T(8,128)S(1)} %fusion.69) | copy-start | bytes 196612
  170.8 7.4 %copy-start.4 = (f32[128,128]{1,0:T(8,128)}, f32[128,128]{1,0:T(8,128)S(1)}, u32[]{:S(2)}) copy-start(f32[128,128]{1,0:T(8,128)S(1)} %fusion.68) | copy-start | bytes 196612
  173.1 7.1 %copy-start.6 = (f32[128,128]{1,0:T(8,128)}, f32[128,128]{1,0:T(8,128)S(1)}, u32[]{:S(2)}) copy-start(f32[128,128]{1,0:T(8,128)S(1)} %fusion.66) | copy-start | bytes 196612
  178.2 72.9 %copy-start.3 = (f32[128,128]{1,0:T(8,128)S(1)}, f32[128,128]{1,0:T(8,128)}, u32[]{:S(2)}) copy-start(f32[128,128]{1,0:T(8,128)} %copy-done.2) | copy-start | bytes 196612
  178.2 76.4 %collective-permute-start.2 = (f32[128,128]{1,0:T(8,128)S(1)}, f32[128,128]{1,0:T(8,128)S(1)}, u32[]{:S(2)}, u32[]{:S(2)}) collective-permute-start(f32[128,128]{1,0:T(8,128)S(1)} %fusion.7), channel_id=1, source_target_pairs={{0,16},{16,0},{32,48},{48,32},{64,80},{80,64},{96,112},{112,96},{1... | collective-permute-start | bytes 196616 | tf_op jit(solution)/shard_map/ppermute | solution.py:16
  180.3 70.8 %copy-start.5 = (f32[128,128]{1,0:T(8,128)S(1)}, f32[128,128]{1,0:T(8,128)}, u32[]{:S(2)}) copy-start(f32[128,128]{1,0:T(8,128)} %copy-done.4) | copy-start | bytes 196612
  235.5 15.6 %copy-start.7 = (f32[128,128]{1,0:T(8,128)S(1)}, f32[128,128]{1,0:T(8,128)}, u32[]{:S(2)}) copy-start(f32[128,128]{1,0:T(8,128)} %copy-done.6) | copy-start | bytes 196612
  235.5 15.6 %copy-start.9 = (f32[128,128]{1,0:T(8,128)S(1)}, f32[128,128]{1,0:T(8,128)}, u32[]{:S(2)}) copy-start(f32[128,128]{1,0:T(8,128)} %copy-done.8) | copy-start | bytes 196612
  243.5 17.9 %copy-start.12 = (f32[512,1]{0,1:T(1,128)S(1)}, f32[512,1]{0,1:T(1,128)}, u32[]{:S(2)}) copy-start(f32[512,1]{0,1:T(1,128)} %get-tuple-element.61) | copy-start | bytes 6148
  245.0 11.7 %collective-permute-start.1 = (f32[128,128]{1,0:T(8,128)S(1)}, f32[128,128]{1,0:T(8,128)S(1)}, u32[]{:S(2)}, u32[]{:S(2)}) collective-permute-start(f32[128,128]{1,0:T(8,128)S(1)} %fusion.34), channel_id=1, source_target_pairs={{0,16},{16,0},{32,48},{48,32},{64,80},{80,64},{96,112},{112,96},{1... | collective-permute-start | bytes 196616 | tf_op jit(solution)/shard_map/ppermute | solution.py:16
  249.2 25.6 %copy-start.11 = (f32[512,1]{0,1:T(1,128)S(1)}, f32[512,1]{0,1:T(1,128)}, u32[]{:S(2)}) copy-start(f32[512,1]{0,1:T(1,128)} %get-tuple-element.60) | copy-start | bytes 6148
  251.1 44.1 %copy-start.10 = (f32[512,1]{0,1:T(1,128)S(1)}, f32[512,1]{0,1:T(1,128)}, u32[]{:S(2)}) copy-start(f32[512,1]{0,1:T(1,128)} %get-tuple-element.59) | copy-start | bytes 6148
  254.8 7.7 %collective-permute-start.4 = (f32[128,128]{1,0:T(8,128)S(1)}, f32[128,128]{1,0:T(8,128)S(1)}, u32[]{:S(2)}, u32[]{:S(2)}) collective-permute-start(f32[128,128]{1,0:T(8,128)S(1)} %fusion.95), channel_id=1, source_target_pairs={{0,32},{16,48},{32,0},{48,16},{64,96},{80,112},{96,64},{112,80},{1... | collective-permute-start | bytes 196616 | tf_op jit(solution)/shard_map/ppermute | solution.py:16
  256.9 14.5 %collective-permute-start.3 = (f32[128,128]{1,0:T(8,128)S(1)}, f32[128,128]{1,0:T(8,128)S(1)}, u32[]{:S(2)}, u32[]{:S(2)}) collective-permute-start(f32[128,128]{1,0:T(8,128)S(1)} %convolution_add_fusion.4), channel_id=1, source_target_pairs={{0,32},{16,48},{32,0},{48,16},{64,96},{80,112},{96,64},{112,80},{1... | collective-permute-start | bytes 196616 | tf_op jit(solution)/shard_map/ppermute | solution.py:16
  262.0 50.7 %copy-start.17 = (f32[128]{0:T(128)S(1)}, f32[128]{0:T(128)}, u32[]{:S(2)}) copy-start(f32[128]{0:T(128)} %param.16) | copy-start | bytes 1540
  262.8 12.7 %collective-permute-start.6 = (f32[128,128]{1,0:T(8,128)S(1)}, f32[128,128]{1,0:T(8,128)S(1)}, u32[]{:S(2)}, u32[]{:S(2)}) collective-permute-start(f32[128,128]{1,0:T(8,128)S(1)} %fusion.90), channel_id=1, source_target_pairs={{0,64},{16,80},{32,96},{48,112},{64,0},{80,16},{96,32},{112,48},{1... | collective-permute-start | bytes 196616 | tf_op jit(solution)/shard_map/ppermute | solution.py:16
  271.7 14.3 %collective-permute-start.5 = (f32[128,128]{1,0:T(8,128)S(1)}, f32[128,128]{1,0:T(8,128)S(1)}, u32[]{:S(2)}, u32[]{:S(2)}) collective-permute-start(f32[128,128]{1,0:T(8,128)S(1)} %convolution_add_fusion.3), channel_id=1, source_target_pairs={{0,64},{16,80},{32,96},{48,112},{64,0},{80,16},{96,32},{112,48},{1... | collective-permute-start | bytes 196616 | tf_op jit(solution)/shard_map/ppermute | solution.py:16
  275.7 20.1 %collective-permute-start.8 = (f32[128,128]{1,0:T(8,128)S(1)}, f32[128,128]{1,0:T(8,128)S(1)}, u32[]{:S(2)}, u32[]{:S(2)}) collective-permute-start(f32[128,128]{1,0:T(8,128)S(1)} %fusion.85), channel_id=1, source_target_pairs={{0,128},{16,144},{32,160},{48,176},{64,192},{80,208},{96,224},{112... | collective-permute-start | bytes 196616 | tf_op jit(solution)/shard_map/ppermute | solution.py:16
  286.2 13.8 %collective-permute-start.7 = (f32[128,128]{1,0:T(8,128)S(1)}, f32[128,128]{1,0:T(8,128)S(1)}, u32[]{:S(2)}, u32[]{:S(2)}) collective-permute-start(f32[128,128]{1,0:T(8,128)S(1)} %convolution_add_fusion.2), channel_id=1, source_target_pairs={{0,128},{16,144},{32,160},{48,176},{64,192},{80,208},{96,224},{112... | collective-permute-start | bytes 196616 | tf_op jit(solution)/shard_map/ppermute | solution.py:16
  296.0 8.2 %collective-permute-start.10 = (f32[128,128]{1,0:T(8,128)S(1)}, f32[128,128]{1,0:T(8,128)S(1)}, u32[]{:S(2)}, u32[]{:S(2)}) collective-permute-start(f32[128,128]{1,0:T(8,128)S(1)} %fusion.80), channel_id=1, source_target_pairs={{0,256},{16,272},{32,288},{48,304},{64,320},{80,336},{96,352},{112... | collective-permute-start | bytes 196616 | tf_op jit(solution)/shard_map/ppermute | solution.py:16
  300.2 5.0 %collective-permute-start.9 = (f32[128,128]{1,0:T(8,128)S(1)}, f32[128,128]{1,0:T(8,128)S(1)}, u32[]{:S(2)}, u32[]{:S(2)}) collective-permute-start(f32[128,128]{1,0:T(8,128)S(1)} %convolution_add_fusion.1), channel_id=1, source_target_pairs={{0,256},{16,272},{32,288},{48,304},{64,320},{80,336},{96,352},{112... | collective-permute-start | bytes 196616 | tf_op jit(solution)/shard_map/ppermute | solution.py:16
  305.5 6.5 %collective-permute-start.11 = (f32[128,128]{1,0:T(8,128)S(1)}, f32[128,128]{1,0:T(8,128)S(1)}, u32[]{:S(2)}, u32[]{:S(2)}) collective-permute-start(f32[128,128]{1,0:T(8,128)S(1)} %convolution_add_fusion), channel_id=1, source_target_pairs={{0,512},{16,528},{32,544},{48,560},{64,576},{80,592},{96,608},{112... | collective-permute-start | bytes 196616 | tf_op jit(solution)/shard_map/ppermute | solution.py:16
  (2 other events, 4.9 us)
Sparse Core Ops, SparseCore 0:
  10.0 75.6 all-gather.1
  318.0 74.1 reduce-scatter.1
where the time goes:
time: 401 us; the launch traced here: 399 us
  waiting for transfers between devices  136 us (34%)
  other arithmetic  87.7 us (22%)
  starting transfers between devices  72.5 us (18%)
  matrix products  54.5 us (14%)
  local copies, waits for them, and re-layouts  33.2 us (8%)
  between operations  14.8 us (4%)
    reduce_scatter x1, waiting for transfers between devices, shards(): lax.psum_scatter(partial_out, 'head', scatter_dimension=1, tiled=True)  74.3 us
    ppermute x11, starting transfers between devices, partner(): return lax.ppermute(value, axis, pairs)  53.4 us
    another operation x3, other arithmetic, shards(): jax.scipy.linalg.solve_triangular(lhs_decay, beta[:, None] * values, lowe...  41.9 us
    another operation x1, other arithmetic, shards(): jax.scipy.linalg.solve_triangular(lhs_plain, beta[:, None] * keys, lower=...  40.7 us
    all_gather x1, waiting for transfers between devices, shards(): portion = lax.all_gather(tokens, 'head', axis=1, tiled=True)  29.6 us
    all_to_all x1, waiting for transfers between devices, shards(): lax.all_to_all(w_out, 'head', split_axis=0, concat_axis=1, tiled=True)  28.1 us
    all_to_all x1, starting transfers between devices, shards(): lax.all_to_all(w_out, 'head', split_axis=0, concat_axis=1, tiled=True)  17.6 us
    another operation x15, local copies, waits for them, and re-layouts, shards(): jax.scipy.linalg.solve_triangular(lhs_decay, beta[:, None] * values, lowe...  15.2 us
  transfers between devices with their start and end apart: 15, of which 7 were waited for; matrix products, arithmetic and copies ran while one was open for 21% of the time, Pallas kernels for 0%

commit v1 on v0

v1 whole, which is shorter than its diff:
```python
import jax
import jax.numpy as jnp
from jax import lax
from jax.experimental import pallas as pl
from jax.experimental.pallas import tpu as pltpu
from jax.sharding import PartitionSpec as P

F32 = jnp.float32
BF16 = jnp.bfloat16
DK = 128
CHUNK = 128
RIM = 8


def split(value):
    high = value.astype(BF16)
    return high, (value - high.astype(F32)).astype(BF16)


def left(value):
    high, low = split(value)
    return jnp.concatenate([high, low], axis=1)


def right(value):
    high, low = split(value)
    both = jnp.concatenate([high, low], axis=1)
    return jnp.concatenate([both, both], axis=0)


def product(lhs, rhs):
    out = jnp.dot(lhs, rhs, preferred_element_type=F32)
    return out[:, :DK] + out[:, DK:]


def softplus(value):
    return jnp.maximum(value, 0.0) + jnp.log1p(jnp.exp(-jnp.abs(value)))


def block_kernel(proj_ref, prior_ref, conv_ref, mix_ref, doc_ref, rate_ref,
                 carried_ref, local_ref, pair_ref, weights_ref, padded_ref):
    rows = proj_ref.shape[0]
    chunks = rows // CHUNK
    width = 3 * DK
    padded_ref[:RIM] = prior_ref[...]
    padded_ref[RIM:] = proj_ref[:, :width]
    row_ids = lax.broadcasted_iota(jnp.int32, (CHUNK, CHUNK), 0)
    col_ids = lax.broadcasted_iota(jnp.int32, (CHUNK, CHUNK), 1)
    lower = row_ids >= col_ids
    strict = row_ids > col_ids
    apart = row_ids ^ col_ids
    identity = (row_ids == col_ids).astype(F32)
    ones_lower = lower.astype(BF16)
    rate = rate_ref[0]
    mix = mix_ref[...]
    level_weights = softplus(mix)
    weights_ref[...] = level_weights
    betas = jax.nn.sigmoid(mix)

    taps = conv_ref[...]
    queries, keys, grams, cross, decays, starts, ends, tails, inverses, lowers = [], [], [], [], [], [], [], [], [], []
    weighted_keys, weighted_values = [], []
    for c in range(chunks):
        base = c * CHUNK
        total = jnp.zeros((CHUNK, width), F32)
        for step in range(4):
            first = base + RIM - 3 + step
            total = total + taps[step:step + 1] * padded_ref[first:first + CHUNK]
        total = total * jax.nn.sigmoid(total)
        q, k, v = total[:, :DK], total[:, DK:2 * DK], total[:, 2 * DK:]
        q = q * lax.rsqrt(jnp.sum(q * q, axis=1, keepdims=True) + 1e-06)
        k = k * lax.rsqrt(jnp.sum(k * k, axis=1, keepdims=True) + 1e-06)
        beta = betas[base:base + CHUNK, 0:1]
        drop = jnp.broadcast_to(-rate * level_weights[base:base + CHUNK, 1:2], (CHUNK, CHUNK))
        high, low = split(drop)
        lowest = (drop - high.astype(F32) - low.astype(F32)).astype(BF16)
        docs = jnp.broadcast_to(doc_ref[base:base + CHUNK], (CHUNK, CHUNK)).astype(BF16)
        sums = jnp.dot(ones_lower, jnp.concatenate([high, low, lowest, docs], axis=1),
                       preferred_element_type=F32)
        drift = sums[:, :CHUNK] + sums[:, CHUNK:2 * CHUNK] + sums[:, 2 * CHUNK:3 * CHUNK]
        count = sums[:, 3 * CHUNK:]
        gap = (drift - drift.T) - 20.0 * (count - count.T)
        decay = jnp.where(lower, jnp.exp(jnp.where(lower, gap, 0.0)), 0.0)
        logs = drift - 20.0 * count
        begin = jnp.exp(logs)
        key_t = right(k.T)
        both = product(left(jnp.concatenate([k, q], axis=0)), key_t)
        queries.append(q)
        keys.append(k)
        grams.append(jnp.where(strict, beta * both[:CHUNK], 0.0))
        cross.append(jnp.where(lower, both[CHUNK:], 0.0))
        decays.append(decay)
        starts.append(begin)
        ends.append(begin[CHUNK - 1:CHUNK])
        tails.append(jnp.exp((drift[CHUNK - 1:CHUNK] - drift) - 20.0 * (count[CHUNK - 1:CHUNK] - count)))
        weighted_keys.append(beta * k)
        weighted_values.append(beta * v)

    inverses = [identity - jnp.where(apart == 1, grams[c], 0.0) for c in range(chunks)]
    size = 2
    while size < CHUNK:
        member = (apart >= size) & (apart < 2 * size)
        rights = [right(inverses[c]) for c in range(chunks)]
        firsts = [product(left(jnp.where(member, grams[c], 0.0)), rights[c]) for c in range(chunks)]
        inverses = [inverses[c] - product(left(inverses[c]), right(firsts[c])) for c in range(chunks)]
        size *= 2

    state = None
    for c in range(chunks):
        base = c * CHUNK
        factor_x = product(left(inverses[c]), right(weighted_keys[c]))
        factor_y = product(left(decays[c] * inverses[c]), right(weighted_values[c]))
        right_x = right(factor_x)
        own = starts[c] * (queries[c] - product(left(cross[c]), right_x))
        near = product(left(decays[c] * cross[c]), right(factor_y))
        right_k = right(keys[c])
        ends_t = jnp.concatenate([factor_x, factor_y * tails[c]], axis=1).T
        ended = product(left(ends_t), right_k)
        trans = ends[c] * (identity - ended[:DK])
        mem = ended[DK:]
        if state is None:
            carried_ref[base:base + CHUNK] = own
            local_ref[base:base + CHUNK] = near
            state = jnp.concatenate([trans, mem], axis=0)
        else:
            own_left = left(own)
            carried_ref[base:base + CHUNK] = product(own_left, right(state[:DK].T))
            local_ref[base:base + CHUNK] = near + product(own_left, right(state[DK:].T))
            moved = product(left(state), right(trans))
            state = jnp.concatenate([moved[:DK], moved[DK:] + mem], axis=0)
    pair_ref[...] = state


def mix_kernel(carried_ref, local_ref, weights_ref, states_ref, gate_ref, gain_ref, out_ref):
    levels = states_ref.shape[0] // DK
    rows = carried_ref.shape[0]
    for base in range(0, rows, CHUNK):
        weights = weights_ref[base:base + CHUNK]
        mixed = weights[:, 2:3] * local_ref[base:base + CHUNK]
        carried = left(carried_ref[base:base + CHUNK])
        for level in range(levels):
            state = states_ref[level * DK:(level + 1) * DK].T
            mixed = mixed + weights[:, level + 3:level + 4] * product(carried, right(state))
        scale = lax.rsqrt(jnp.mean(mixed * mixed, axis=1, keepdims=True) + 1e-05)
        gate = gate_ref[base:base + CHUNK]
        out_ref[base:base + CHUNK] = mixed * scale * gain_ref[...] * (gate * jax.nn.sigmoid(gate))


def shifted(value, axis, steps):
    count = lax.axis_size(axis)
    initial, last = (max(0, -steps), min(count, count - steps))
    return lax.ppermute(value, axis, [(source, source + steps) for source in range(initial, last)])


def partner(value, axis, bit):
    mask = 2**bit
    pairs = [(source, source ^ mask) for source in range(lax.axis_size(axis))]
    return lax.ppermute(value, axis, pairs)


VMEM = pl.BlockSpec(memory_space=pltpu.VMEM)
SMEM = pl.BlockSpec(memory_space=pltpu.SMEM)


def shards(tokens, w_proj, w_mix, conv_w, rates, doc_start, norm_gain, w_out):
    high = lax.Precision.HIGH
    highest = lax.Precision.HIGHEST
    rows = tokens.shape[0]
    portion = lax.all_gather(tokens, "head", axis=1, tiled=True)
    projected = jnp.dot(portion, w_proj, precision=high, preferred_element_type=F32)
    padded_mix = jnp.pad(w_mix, ((0, 0), (0, DK - w_mix.shape[1])))
    mixing = jnp.dot(portion, padded_mix, precision=high, preferred_element_type=F32)
    prior = shifted(projected[rows - RIM:, :3 * DK], "ctx", 1)
    carried, local, pair, weights = pl.pallas_call(
        block_kernel,
        out_shape=[
            jax.ShapeDtypeStruct((rows, DK), F32),
            jax.ShapeDtypeStruct((rows, DK), F32),
            jax.ShapeDtypeStruct((2 * DK, DK), F32),
            jax.ShapeDtypeStruct((rows, DK), F32),
        ],
        in_specs=[VMEM, VMEM, VMEM, VMEM, VMEM, SMEM],
        out_specs=[VMEM] * 4,
        scratch_shapes=[pltpu.VMEM((rows + RIM, 3 * DK), F32)],
        compiler_params=pltpu.CompilerParams(vmem_limit_bytes=48 << 20),
        name="block",
    )(projected, prior, conv_w, mixing, doc_start.astype(F32)[:, None], rates)
    my_index = lax.axis_index("ctx")
    nbits = lax.axis_size("ctx").bit_length() - 1
    group_a, group_b = pair[:DK], pair[DK:]
    identity_d = jnp.eye(DK, dtype=F32)
    carry_m = identity_d
    level_states = []
    for level in range(nbits):
        other_a, other_b = partner((group_a, group_b), "ctx", level)
        upper = my_index >> level & 1 == 1
        seg_a = jnp.where(upper, other_a, identity_d)
        seg_b = jnp.where(upper, other_b, 0.0)
        first_a = jnp.where(upper, other_a, group_a)
        first_b = jnp.where(upper, other_b, group_b)
        second_a = jnp.where(upper, group_a, other_a)
        second_b = jnp.where(upper, group_b, other_b)
        group_a = jnp.dot(first_a, second_a, precision=highest, preferred_element_type=F32)
        group_b = jnp.dot(first_b, second_a, precision=highest, preferred_element_type=F32) + second_b
        level_states.append(jnp.dot(seg_b, carry_m, precision=highest, preferred_element_type=F32))
        carry_m = jnp.dot(seg_a, carry_m, precision=highest, preferred_element_type=F32)
    normed = pl.pallas_call(
        mix_kernel,
        out_shape=jax.ShapeDtypeStruct((rows, DK), F32),
        in_specs=[VMEM] * 6,
        out_specs=VMEM,
        name="mix",
    )(carried, local, weights, jnp.concatenate(level_states, axis=0), projected[:, 3 * DK:],
      norm_gain[None, :])
    every = lax.all_gather(normed, "head", axis=1, tiled=True)
    return jnp.dot(every, w_out, precision=high, preferred_element_type=F32)


def solution(mesh):
    placed = (
        P("ctx", "head"),
        P(None, "head"),
        P(None, "head"),
        P(None, "head"),
        P("head"),
        P("ctx"),
        P("head"),
        P(None, "head"),
    )
    return jax.shard_map(
        shards, mesh=mesh, in_specs=placed, out_specs=P("ctx", "head"), check_vma=False
    )
```

time: 401 us -> 236 us (0.59)
  other arithmetic: 87.7 us -> 0.68 us
  matrix products: 54.5 us -> 17.9 us
  local copies, waits for them, and re-layouts: 33.2 us -> 3.76 us
  starting transfers between devices: 72.5 us -> 56.8 us
  Pallas kernels: 0 us -> 8.68 us
    another operation x7 -> x0, other arithmetic: 83 us -> none  [the longest x3 41.9 us: shards(): jax.scipy.linalg.solve_triangular(lhs_decay, beta[:, None] * values, lowe...]
    reduce_scatter x1 -> x0, waiting for transfers between devices: 74.3 us -> none  [shards(): lax.psum_scatter(partial_out, 'head', scatter_dimension=1, tiled=True)]
    all_gather x0 -> x1, waiting for transfers between devices: none -> 54.5 us  [shards(): every = lax.all_gather(normed, 'head', axis=1, tiled=True)]
    all_gather x1, waiting for transfers between devices: 29.6 us -> 67.2 us  [shards(): portion = lax.all_gather(tokens, 'head', axis=1, tiled=True)]
    another operation x29 -> x0, local copies, waits for them, and re-layouts: 29.4 us -> none  [the longest x15 15.2 us: shards(): jax.scipy.linalg.solve_triangular(lhs_decay, beta[:, None] * values, lowe...]
    all_to_all x1 -> x0, waiting for transfers between devices: 28.1 us -> none  [shards(): lax.all_to_all(w_out, 'head', split_axis=0, concat_axis=1, tiled=True)]
    dot_general x35 -> x23, matrix products: 38.5 us -> 17.9 us  [the longest x1 7.34 us: shards(): jnp.dot(portion, w_proj, precision=high, preferred_element_type=F32)]
    all_to_all x1 -> x0, starting transfers between devices: 17.6 us -> none  [shards(): lax.all_to_all(w_out, 'head', split_axis=0, concat_axis=1, tiled=True)]
  transfers between devices with their start and end apart: 15 -> 14, of which waited for: 7 -> 5; matrix products, arithmetic and copies ran while one was open for 21% -> 3% of each run, Pallas kernels for 0% -> 0%
where the time goes in v1:
time: 236 us; the launch traced here: 235 us
  waiting for transfers between devices  133 us (56%)
  starting transfers between devices  56.8 us (24%)
  matrix products  17.9 us (8%)
  between operations  14.5 us (6%)
  Pallas kernels  8.68 us (4%)
  local copies, waits for them, and re-layouts  3.76 us (2%)
    all_gather x1, waiting for transfers between devices, shards(): portion = lax.all_gather(tokens, 'head', axis=1, tiled=True)  67.2 us
    all_gather x1, waiting for transfers between devices, shards(): every = lax.all_gather(normed, 'head', axis=1, tiled=True)  54.5 us
    ppermute x11, starting transfers between devices, partner(): return lax.ppermute(value, axis, pairs)  54 us
    ppermute x11, waiting for transfers between devices, partner(): return lax.ppermute(value, axis, pairs)  10.6 us
    dot_general x1, matrix products, shards(): jnp.dot(portion, w_proj, precision=high, preferred_element_type=F32)  7.34 us
    pallas_call x1, Pallas kernels, shards(): pl.pallas_call(block_kernel, out_shape=[jax.ShapeDtypeStruct((rows, DK),...  4.77 us
  transfers between devices with their start and end apart: 14, of which 5 were waited for; matrix products, arithmetic and copies ran while one was open for 3% of the time, Pallas kernels for 0%

profile of v1, /device:TPU:1, one launch (start us, length us, event | category | flops | bytes accessed | tf_op | source)
XLA Modules:
  0.0 235.3 jit_solution(8910882502958735173)
XLA Ops:
  6.5 0.7 all-gather.3.cloned.1.call-update
  7.3 0.7 convert_element_type.16
  8.8 67.2 %all-gather.3.cloned.1.call-done = f32[512,2048]{1,0:T(8,128)} async-done(((f32[512,128]{1,0:T(8,128)}), f32[512,2048]{1,0:T(8,128)}) %all-gather.3.cloned.1.call-update) | async-done | bytes 4194320 | tf_op jit(solution)/shard_map/all_gather | solution.py:169
  76.0 7.3 %fusion.63.proj_ref = f32[512,512]{1,0:T(8,128)S(1)} fusion(f32[512,2048]{1,0:T(8,128)} %all-gather.3.cloned.1.call-done, f32[2048,512]{1,0:T(8,128)} %param.9), kind=kOutput, calls=%fused_computation.85 | convolution fusion | flops 3221225472 | bytes 9437184 | tf_op jit(solution)/shard_map/dot_general | solution.py:170
  83.4 2.7 %collective-permute-start = (f32[8,384]{1,0:T(8,128)S(1)}, f32[8,384]{1,0:T(8,128)S(1)}, u32[]{:S(2)}, u32[]{:S(2)}) collective-permute-start(f32[8,384]{1,0:T(8,128)S(1)} %slice.16), channel_id=1, source_target_pairs={{0,16},{16,32},{32,48},{48,64},{64,80},{80,96},{96,112},{112,128},... | collective-permute-start | bytes 36872 | tf_op jit(solution)/shard_map/ppermute | solution.py:152
  86.2 1.8 convolution_bitcast_fusion.mix_ref
  88.0 4.8 %block.1 = (f32[512,128]{1,0:T(8,128)S(1)}, f32[512,128]{1,0:T(8,128)S(1)}, f32[256,128]{1,0:T(8,128)S(1)}, f32[512,128]{1,0:T(8,128)S(1)}) custom-call(f32[512,512]{1,0:T(8,128)S(1)} %fusion.63.proj_ref, f32[8,384]{1,0:T(8,128)S(1)} %collective-permute-done.prior_ref, f32[4,384]{1,0:T(4,128)S(1)} %copy-done.4, ...), custom_call_target="tpu_custom_call" | custom-call | tf_op jit(solution)/shard_map/block/pallas_call | solution.py:174
  92.8 0.7 copy-done.1
  93.5 0.7 copy-done.2
  94.2 0.7 copy-done.3
  94.9 3.3 %collective-permute-start.2 = (f32[128,128]{1,0:T(8,128)S(1)}, f32[128,128]{1,0:T(8,128)S(1)}, u32[]{:S(2)}, u32[]{:S(2)}) collective-permute-start(f32[128,128]{1,0:T(8,128)S(1)} %get-tuple-element.13), channel_id=1, source_target_pairs={{0,16},{16,0},{32,48},{48,32},{64,80},{80,64},{96,112},{112,96},{1... | collective-permute-start | bytes 196616 | tf_op jit(solution)/shard_map/ppermute | solution.py:158
  98.2 0.8 slice.17.gate_ref
  98.9 2.0 collective-permute-start.1
  101.1 5.5 %collective-permute-start.4 = (f32[128,128]{1,0:T(8,128)S(1)}, f32[128,128]{1,0:T(8,128)S(1)}, u32[]{:S(2)}, u32[]{:S(2)}) collective-permute-start(f32[128,128]{1,0:T(8,128)S(1)} %fusion.20), channel_id=1, source_target_pairs={{0,32},{16,48},{32,0},{48,16},{64,96},{80,112},{96,64},{112,80},{1... | collective-permute-start | bytes 196616 | tf_op jit(solution)/shard_map/ppermute | solution.py:158
  106.7 0.2 convolution_add_fusion.4
  106.9 2.8 %collective-permute-start.3 = (f32[128,128]{1,0:T(8,128)S(1)}, f32[128,128]{1,0:T(8,128)S(1)}, u32[]{:S(2)}, u32[]{:S(2)}) collective-permute-start(f32[128,128]{1,0:T(8,128)S(1)} %convolution_add_fusion.4), channel_id=1, source_target_pairs={{0,32},{16,48},{32,0},{48,16},{64,96},{80,112},{96,64},{112,80},{1... | collective-permute-start | bytes 196616 | tf_op jit(solution)/shard_map/ppermute | solution.py:158
  110.3 7.7 %collective-permute-start.6 = (f32[128,128]{1,0:T(8,128)S(1)}, f32[128,128]{1,0:T(8,128)S(1)}, u32[]{:S(2)}, u32[]{:S(2)}) collective-permute-start(f32[128,128]{1,0:T(8,128)S(1)} %fusion.16), channel_id=1, source_target_pairs={{0,64},{16,80},{32,96},{48,112},{64,0},{80,16},{96,32},{112,48},{1... | collective-permute-start | bytes 196616 | tf_op jit(solution)/shard_map/ppermute | solution.py:158
  118.1 0.2 convolution_add_fusion.3
  118.3 2.4 %collective-permute-start.5 = (f32[128,128]{1,0:T(8,128)S(1)}, f32[128,128]{1,0:T(8,128)S(1)}, u32[]{:S(2)}, u32[]{:S(2)}) collective-permute-start(f32[128,128]{1,0:T(8,128)S(1)} %convolution_add_fusion.3), channel_id=1, source_target_pairs={{0,64},{16,80},{32,96},{48,112},{64,0},{80,16},{96,32},{112,48},{1... | collective-permute-start | bytes 196616 | tf_op jit(solution)/shard_map/ppermute | solution.py:158
  121.4 16.1 %collective-permute-start.8 = (f32[128,128]{1,0:T(8,128)S(1)}, f32[128,128]{1,0:T(8,128)S(1)}, u32[]{:S(2)}, u32[]{:S(2)}) collective-permute-start(f32[128,128]{1,0:T(8,128)S(1)} %fusion.12), channel_id=1, source_target_pairs={{0,128},{16,144},{32,160},{48,176},{64,192},{80,208},{96,224},{112... | collective-permute-start | bytes 196616 | tf_op jit(solution)/shard_map/ppermute | solution.py:158
  137.5 0.2 convolution_add_fusion.2
  137.7 3.3 %collective-permute-start.7 = (f32[128,128]{1,0:T(8,128)S(1)}, f32[128,128]{1,0:T(8,128)S(1)}, u32[]{:S(2)}, u32[]{:S(2)}) collective-permute-start(f32[128,128]{1,0:T(8,128)S(1)} %convolution_add_fusion.2), channel_id=1, source_target_pairs={{0,128},{16,144},{32,160},{48,176},{64,192},{80,208},{96,224},{112... | collective-permute-start | bytes 196616 | tf_op jit(solution)/shard_map/ppermute | solution.py:158
  141.7 3.1 %collective-permute-start.10 = (f32[128,128]{1,0:T(8,128)S(1)}, f32[128,128]{1,0:T(8,128)S(1)}, u32[]{:S(2)}, u32[]{:S(2)}) collective-permute-start(f32[128,128]{1,0:T(8,128)S(1)} %fusion.8), channel_id=1, source_target_pairs={{0,256},{16,272},{32,288},{48,304},{64,320},{80,336},{96,352},{112... | collective-permute-start | bytes 196616 | tf_op jit(solution)/shard_map/ppermute | solution.py:158
  144.7 7.4 %collective-permute-done.7 = f32[128,128]{1,0:T(8,128)S(1)} collective-permute-done((f32[128,128]{1,0:T(8,128)S(1)}, f32[128,128]{1,0:T(8,128)S(1)}, u32[]{:S(2)}, u32[]{:S(2)}) %collective-permute-start.7) | collective-permute-done | bytes 65568 | tf_op jit(solution)/shard_map/ppermute | solution.py:158
  152.3 3.0 %collective-permute-start.9 = (f32[128,128]{1,0:T(8,128)S(1)}, f32[128,128]{1,0:T(8,128)S(1)}, u32[]{:S(2)}, u32[]{:S(2)}) collective-permute-start(f32[128,128]{1,0:T(8,128)S(1)} %convolution_add_fusion.1), channel_id=1, source_target_pairs={{0,256},{16,272},{32,288},{48,304},{64,320},{80,336},{96,352},{112... | collective-permute-start | bytes 196616 | tf_op jit(solution)/shard_map/ppermute | solution.py:158
  155.8 1.5 collective-permute-done.9
  157.5 4.8 %collective-permute-start.11 = (f32[128,128]{1,0:T(8,128)S(1)}, f32[128,128]{1,0:T(8,128)S(1)}, u32[]{:S(2)}, u32[]{:S(2)}) collective-permute-start(f32[128,128]{1,0:T(8,128)S(1)} %convolution_add_fusion), channel_id=1, source_target_pairs={{0,512},{16,528},{32,544},{48,560},{64,576},{80,592},{96,608},{112... | collective-permute-start | bytes 196616 | tf_op jit(solution)/shard_map/ppermute | solution.py:158
  162.7 1.6 collective-permute-done.11
  164.6 0.7 copy-done.6
  165.3 3.9 %mix.1 = f32[512,128]{1,0:T(8,128)} custom-call(f32[512,128]{1,0:T(8,128)} %copy-done.1, f32[512,128]{1,0:T(8,128)} %copy-done.2, f32[512,128]{1,0:T(8,128)} %copy-done.3, f32[768,128]{1,0:T(8,128)} %copy-done.6, f32[512,128]{1,0:T(8,128)} %slice.17.gate_ref, f32[1,128]{1,0:T(1,128)} %bitcast.19), custom_call_target="tpu_custom_call" | custom-call | tf_op jit(solution)/shard_map/mix/pallas_call | solution.py:207
  169.3 54.5 %all-gather.5.cloned.1.call-done = f32[512,2048]{1,0:T(8,128)} async-done(((f32[512,128]{1,0:T(8,128)}), f32[512,2048]{1,0:T(8,128)}) %all-gather.5.cloned.1.call-update) | async-done | bytes 4194320 | tf_op jit(solution)/shard_map/all_gather | solution.py:215
  223.7 4.7 %fusion.64 = f32[512,128]{1,0:T(8,128)} fusion(f32[512,2048]{1,0:T(8,128)} %all-gather.5.cloned.1.call-done, f32[2048,128]{1,0:T(8,128)S(1)} %copy-done), kind=kOutput, calls=%fused_computation.86 | convolution fusion | flops 805306368 | bytes 5505024 | tf_op jit(solution)/shard_map/dot_general | solution.py:216
  (44 shorter events, 3.7 us)
Async XLA Ops:
  6.5 217.2 %copy-start = (f32[2048,128]{1,0:T(8,128)S(1)}, f32[2048,128]{1,0:T(8,128)}, u32[]{:S(2)}) copy-start(f32[2048,128]{1,0:T(8,128)} %param.15) | copy-start | bytes 3145732
  6.5 69.5 %all-gather.3.cloned.1.call-start = ((), (), s32[]{:S(2)}) async-start(), calls=%async_computation | async-start | bytes 4456448 | tf_op jit(solution)/shard_map/all_gather | solution.py:169
  7.3 216.5 %all-gather.5.cloned.1.call-start = ((), (), s32[]{:S(2)}) async-start(), calls=%async_computation.1 | async-start | bytes 4456448 | tf_op jit(solution)/shard_map/all_gather | solution.py:215
  8.8 77.3 %copy-start.7 = (f32[2048,9]{0,1:T(8,128)S(1)}, f32[2048,9]{0,1:T(8,128)}, u32[]{:S(2)}) copy-start(f32[2048,9]{0,1:T(8,128)} %param.10) | copy-start | bytes 221188
  76.0 10.1 %copy-start.5 = (f32[512,2048]{1,0:T(8,128)S(1)}, f32[512,2048]{1,0:T(8,128)}, u32[]{:S(2)}) copy-start(f32[512,2048]{1,0:T(8,128)} %all-gather.3.cloned.1.call-done) | copy-start | bytes 12582916
  83.4 4.6 %copy-start.4 = (f32[4,384]{1,0:T(4,128)S(1)}, f32[4,384]{1,0:T(4,128)}, u32[]{:S(2)}) copy-start(f32[4,384]{1,0:T(4,128)} %conv_ref.1) | copy-start | bytes 18436
  83.4 4.5 %collective-permute-start = (f32[8,384]{1,0:T(8,128)S(1)}, f32[8,384]{1,0:T(8,128)S(1)}, u32[]{:S(2)}, u32[]{:S(2)}) collective-permute-start(f32[8,384]{1,0:T(8,128)S(1)} %slice.16), channel_id=1, source_target_pairs={{0,16},{16,32},{32,48},{48,64},{64,80},{80,96},{96,112},{112,128},... | collective-permute-start | bytes 36872 | tf_op jit(solution)/shard_map/ppermute | solution.py:152
  92.8 0.7 copy-start.1
  93.5 0.7 copy-start.2
  94.2 0.7 copy-start.3
  94.9 6.1 %collective-permute-start.2 = (f32[128,128]{1,0:T(8,128)S(1)}, f32[128,128]{1,0:T(8,128)S(1)}, u32[]{:S(2)}, u32[]{:S(2)}) collective-permute-start(f32[128,128]{1,0:T(8,128)S(1)} %get-tuple-element.13), channel_id=1, source_target_pairs={{0,16},{16,0},{32,48},{48,32},{64,80},{80,64},{96,112},{112,96},{1... | collective-permute-start | bytes 196616 | tf_op jit(solution)/shard_map/ppermute | solution.py:158
  98.9 7.7 %collective-permute-start.1 = (f32[128,128]{1,0:T(8,128)S(1)}, f32[128,128]{1,0:T(8,128)S(1)}, u32[]{:S(2)}, u32[]{:S(2)}) collective-permute-start(f32[128,128]{1,0:T(8,128)S(1)} %get-tuple-element.14), channel_id=1, source_target_pairs={{0,16},{16,0},{32,48},{48,32},{64,80},{80,64},{96,112},{112,96},{1... | collective-permute-start | bytes 196616 | tf_op jit(solution)/shard_map/ppermute | solution.py:158
  101.1 8.9 %collective-permute-start.4 = (f32[128,128]{1,0:T(8,128)S(1)}, f32[128,128]{1,0:T(8,128)S(1)}, u32[]{:S(2)}, u32[]{:S(2)}) collective-permute-start(f32[128,128]{1,0:T(8,128)S(1)} %fusion.20), channel_id=1, source_target_pairs={{0,32},{16,48},{32,0},{48,16},{64,96},{80,112},{96,64},{112,80},{1... | collective-permute-start | bytes 196616 | tf_op jit(solution)/shard_map/ppermute | solution.py:158
  106.9 11.2 %collective-permute-start.3 = (f32[128,128]{1,0:T(8,128)S(1)}, f32[128,128]{1,0:T(8,128)S(1)}, u32[]{:S(2)}, u32[]{:S(2)}) collective-permute-start(f32[128,128]{1,0:T(8,128)S(1)} %convolution_add_fusion.4), channel_id=1, source_target_pairs={{0,32},{16,48},{32,0},{48,16},{64,96},{80,112},{96,64},{112,80},{1... | collective-permute-start | bytes 196616 | tf_op jit(solution)/shard_map/ppermute | solution.py:158
  110.3 10.8 %collective-permute-start.6 = (f32[128,128]{1,0:T(8,128)S(1)}, f32[128,128]{1,0:T(8,128)S(1)}, u32[]{:S(2)}, u32[]{:S(2)}) collective-permute-start(f32[128,128]{1,0:T(8,128)S(1)} %fusion.16), channel_id=1, source_target_pairs={{0,64},{16,80},{32,96},{48,112},{64,0},{80,16},{96,32},{112,48},{1... | collective-permute-start | bytes 196616 | tf_op jit(solution)/shard_map/ppermute | solution.py:158
  118.3 19.2 %collective-permute-start.5 = (f32[128,128]{1,0:T(8,128)S(1)}, f32[128,128]{1,0:T(8,128)S(1)}, u32[]{:S(2)}, u32[]{:S(2)}) collective-permute-start(f32[128,128]{1,0:T(8,128)S(1)} %convolution_add_fusion.3), channel_id=1, source_target_pairs={{0,64},{16,80},{32,96},{48,112},{64,0},{80,16},{96,32},{112,48},{1... | collective-permute-start | bytes 196616 | tf_op jit(solution)/shard_map/ppermute | solution.py:158
  121.4 20.1 %collective-permute-start.8 = (f32[128,128]{1,0:T(8,128)S(1)}, f32[128,128]{1,0:T(8,128)S(1)}, u32[]{:S(2)}, u32[]{:S(2)}) collective-permute-start(f32[128,128]{1,0:T(8,128)S(1)} %fusion.12), channel_id=1, source_target_pairs={{0,128},{16,144},{32,160},{48,176},{64,192},{80,208},{96,224},{112... | collective-permute-start | bytes 196616 | tf_op jit(solution)/shard_map/ppermute | solution.py:158
  137.7 14.4 %collective-permute-start.7 = (f32[128,128]{1,0:T(8,128)S(1)}, f32[128,128]{1,0:T(8,128)S(1)}, u32[]{:S(2)}, u32[]{:S(2)}) collective-permute-start(f32[128,128]{1,0:T(8,128)S(1)} %convolution_add_fusion.2), channel_id=1, source_target_pairs={{0,128},{16,144},{32,160},{48,176},{64,192},{80,208},{96,224},{112... | collective-permute-start | bytes 196616 | tf_op jit(solution)/shard_map/ppermute | solution.py:158
  141.7 14.1 %collective-permute-start.10 = (f32[128,128]{1,0:T(8,128)S(1)}, f32[128,128]{1,0:T(8,128)S(1)}, u32[]{:S(2)}, u32[]{:S(2)}) collective-permute-start(f32[128,128]{1,0:T(8,128)S(1)} %fusion.8), channel_id=1, source_target_pairs={{0,256},{16,272},{32,288},{48,304},{64,320},{80,336},{96,352},{112... | collective-permute-start | bytes 196616 | tf_op jit(solution)/shard_map/ppermute | solution.py:158
  152.3 5.0 %collective-permute-start.9 = (f32[128,128]{1,0:T(8,128)S(1)}, f32[128,128]{1,0:T(8,128)S(1)}, u32[]{:S(2)}, u32[]{:S(2)}) collective-permute-start(f32[128,128]{1,0:T(8,128)S(1)} %convolution_add_fusion.1), channel_id=1, source_target_pairs={{0,256},{16,272},{32,288},{48,304},{64,320},{80,336},{96,352},{112... | collective-permute-start | bytes 196616 | tf_op jit(solution)/shard_map/ppermute | solution.py:158
  157.5 6.8 %collective-permute-start.11 = (f32[128,128]{1,0:T(8,128)S(1)}, f32[128,128]{1,0:T(8,128)S(1)}, u32[]{:S(2)}, u32[]{:S(2)}) collective-permute-start(f32[128,128]{1,0:T(8,128)S(1)} %convolution_add_fusion), channel_id=1, source_target_pairs={{0,512},{16,528},{32,544},{48,560},{64,576},{80,592},{96,608},{112... | collective-permute-start | bytes 196616 | tf_op jit(solution)/shard_map/ppermute | solution.py:158
  164.6 0.7 copy-start.6
Sparse Core Ops, SparseCore 0:
  10.0 66.0 all-gather.2
  169.4 54.2 all-gather.4

commit v2 on v1

--- a/solution.py
+++ b/solution.py
@@ -1,3 +1,5 @@
+import functools
+
 import jax
 import jax.numpy as jnp
 from jax import lax
@@ -10,6 +12,9 @@
 DK = 128
 CHUNK = 128
 RIM = 8
+MESH = pl.DeviceIdType.MESH
+VMEM = pl.BlockSpec(memory_space=pltpu.VMEM)
+SMEM = pl.BlockSpec(memory_space=pltpu.SMEM)
 
 
 def split(value):
@@ -146,6 +151,168 @@
         out_ref[base:base + CHUNK] = mixed * scale * gain_ref[...] * (gate * jax.nn.sigmoid(gate))
 
 
+PARTS = 4
+
+
+def gather_kernel(x_ref, *refs, sizes):
+    count = len(sizes)
+    weight_refs, out_refs = refs[:count], refs[count:2 * count]
+    held, store, load_sem, send_sem, recv_sem, near_send, near_recv = refs[2 * count:]
+    heads = held.shape[0]
+    chips = heads // 2
+    half = chips // 2
+    rows = x_ref.shape[0]
+    part = rows // PARTS
+    me = lax.axis_index("head")
+    chip, core = me // 2, me % 2
+    sibling = me + 1 - 2 * core
+    targets = (
+        lax.rem(chip + 1, chips) * 2 + core,
+        lax.rem(chip + chips - 1, chips) * 2 + core,
+    )
+    load = pltpu.make_async_copy(weight_refs[0], store, load_sem)
+    load.start()
+    barrier = pltpu.get_barrier_semaphore()
+    for neighbour in (*targets, sibling):
+        pl.semaphore_signal(barrier, inc=1, device_id={"head": neighbour}, device_id_type=MESH)
+    pl.semaphore_wait(barrier, 3)
+
+    def slot_of(direction, hop):
+        offset = chips - hop if direction == 0 else hop
+        return lax.rem(chip + offset, chips) * 2 + core
+
+    def span(index):
+        return pl.ds(index * part, part)
+
+    def ring(direction, hop, index):
+        slot = slot_of(direction, hop)
+        return pltpu.make_async_remote_copy(
+            src_ref=held.at[slot, span(index)],
+            dst_ref=held.at[slot, span(index)],
+            send_sem=send_sem.at[direction, hop, index],
+            recv_sem=recv_sem.at[direction, hop, index],
+            device_id={"head": targets[direction]},
+            device_id_type=MESH,
+        )
+
+    def first(direction, index):
+        return pltpu.make_async_remote_copy(
+            src_ref=x_ref.at[span(index)],
+            dst_ref=held.at[me, span(index)],
+            send_sem=send_sem.at[direction, 0, index],
+            recv_sem=recv_sem.at[direction, 0, index],
+            device_id={"head": targets[direction]},
+            device_id_type=MESH,
+        )
+
+    def near(slot, offset, index, source):
+        return pltpu.make_async_remote_copy(
+            src_ref=source.at[span(index)],
+            dst_ref=held.at[slot, span(index)],
+            send_sem=near_send.at[offset, index],
+            recv_sem=near_recv.at[offset, index],
+            device_id={"head": sibling},
+            device_id_type=MESH,
+        )
+
+    def goes(direction, hop, index):
+        longest = half if (index < PARTS // 2) == (direction == 0) else half - 1
+        return hop <= longest
+
+    for index in range(PARTS):
+        for direction in range(2):
+            if goes(direction, 1, index):
+                first(direction, index).start()
+    for index in range(PARTS):
+        near(me, 0, index, x_ref).start()
+    held[me] = x_ref[...]
+    for ref in out_refs:
+        ref[...] = jnp.zeros_like(ref)
+    load.wait()
+
+    def step(hop, carry):
+        for index in range(PARTS):
+            for direction in range(2):
+                @pl.when((hop >= 1) & goes(direction, hop, index))
+                def _():
+                    ring(direction, hop - 1, index).wait_recv()
+
+                @pl.when((hop >= 1) & goes(direction, hop + 1, index))
+                def _():
+                    ring(direction, hop, index).start()
+
+                @pl.when((hop >= 1) & goes(direction, hop, index))
+                def _():
+                    slot = slot_of(direction, hop)
+                    offset = chips - hop if direction == 0 else hop
+                    near(slot, offset, index, held.at[slot]).start()
+
+        def block(which, inner):
+            offset = jnp.where(which == 0, hop, chips - hop)
+            offset = lax.rem(offset, chips)
+            there = lax.rem(chip + offset, chips)
+            for index in range(PARTS):
+                other = there * 2 + 1 - core
+                near(other, offset, index, held.at[other]).wait_recv()
+            lhs = jnp.concatenate([held[there * 2], held[there * 2 + 1]], axis=1)
+            lhs_high, lhs_low = split(lhs)
+            begin = pl.multiple_of(there * 2 * DK, 2 * DK)
+            for number, ref in enumerate(out_refs):
+                source = store if number == 0 else weight_refs[number]
+                high, low = split(source[pl.ds(begin, 2 * DK), :])
+                width = high.shape[1]
+                if width == DK:
+                    both = jnp.concatenate([high, low], axis=1)
+                    out = jnp.dot(lhs_high, both, preferred_element_type=F32)
+                    ref[...] += out[:, :DK] + out[:, DK:] + jnp.dot(lhs_low, high, preferred_element_type=F32)
+                else:
+                    ref[...] += (
+                        jnp.dot(lhs_high, high, preferred_element_type=F32)
+                        + jnp.dot(lhs_high, low, preferred_element_type=F32)
+                        + jnp.dot(lhs_low, high, preferred_element_type=F32)
+                    )
+            return inner
+
+        lax.fori_loop(0, jnp.where((hop == 0) | (hop == half), 1, 2), block, 0)
+        return carry
+
+    lax.fori_loop(0, half + 1, step, 0)
+
+    for index in range(PARTS):
+        for direction in range(2):
+            for hop in range(half):
+                if goes(direction, hop + 1, index):
+                    ring(direction, hop, index).wait_send()
+        for offset in range(chips):
+            near(me, offset, index, x_ref).wait_send()
+
+
+def gather_matmul(values, weights, collective_id, name):
+    rows = values.shape[0]
+    heads = lax.axis_size("head")
+    sizes = tuple(weight.shape[1] for weight in weights)
+    half = heads // 4
+    return pl.pallas_call(
+        functools.partial(gather_kernel, sizes=sizes),
+        out_shape=[jax.ShapeDtypeStruct((rows, size), F32) for size in sizes],
+        in_specs=[VMEM, pl.BlockSpec(memory_space=pl.ANY)] + [VMEM] * (len(sizes) - 1),
+        out_specs=[VMEM] * len(sizes),
+        scratch_shapes=[
+            pltpu.VMEM((heads, rows, DK), F32),
+            pltpu.VMEM(weights[0].shape, F32),
+            pltpu.SemaphoreType.DMA,
+            pltpu.SemaphoreType.DMA((2, half, PARTS)),
+            pltpu.SemaphoreType.DMA((2, half, PARTS)),
+            pltpu.SemaphoreType.DMA((heads // 2, PARTS)),
+            pltpu.SemaphoreType.DMA((heads // 2, PARTS)),
+        ],
+        compiler_params=pltpu.CompilerParams(
+            collective_id=collective_id, has_side_effects=True, vmem_limit_bytes=48 << 20
+        ),
+        name=name,
+    )(values, *weights)
+
+
 def shifted(value, axis, steps):
     count = lax.axis_size(axis)
     initial, last = (max(0, -steps), min(count, count - steps))
@@ -158,18 +325,10 @@
     return lax.ppermute(value, axis, pairs)
 
 
-VMEM = pl.BlockSpec(memory_space=pltpu.VMEM)
-SMEM = pl.BlockSpec(memory_space=pltpu.SMEM)
-
-
 def shards(tokens, w_proj, w_mix, conv_w, rates, doc_start, norm_gain, w_out):
-    high = lax.Precision.HIGH
     highest = lax.Precision.HIGHEST
     rows = tokens.shape[0]
-    portion = lax.all_gather(tokens, "head", axis=1, tiled=True)
-    projected = jnp.dot(portion, w_proj, precision=high, preferred_element_type=F32)
-    padded_mix = jnp.pad(w_mix, ((0, 0), (0, DK - w_mix.shape[1])))
-    mixing = jnp.dot(portion, padded_mix, precision=high, preferred_element_type=F32)
+    projected, mixing = gather_matmul(tokens, [w_proj, w_mix], 0, "project")
     prior = shifted(projected[rows - RIM:, :3 * DK], "ctx", 1)
     carried, local, pair, weights = pl.pallas_call(
         block_kernel,
@@ -177,7 +336,7 @@
             jax.ShapeDtypeStruct((rows, DK), F32),
             jax.ShapeDtypeStruct((rows, DK), F32),
             jax.ShapeDtypeStruct((2 * DK, DK), F32),
-            jax.ShapeDtypeStruct((rows, DK), F32),
+            jax.ShapeDtypeStruct(mixing.shape, F32),
         ],
         in_specs=[VMEM, VMEM, VMEM, VMEM, VMEM, SMEM],
         out_specs=[VMEM] * 4,
@@ -212,8 +371,7 @@
         name="mix",
     )(carried, local, weights, jnp.concatenate(level_states, axis=0), projected[:, 3 * DK:],
       norm_gain[None, :])
-    every = lax.all_gather(normed, "head", axis=1, tiled=True)
-    return jnp.dot(every, w_out, precision=high, preferred_element_type=F32)
+    return gather_matmul(normed, [w_out], 1, "combine")[0]
 
 
 def solution(mesh):

time: 236 us -> 158 us (0.67)
  waiting for transfers between devices: 133 us -> 4.15 us
  Pallas kernels: 8.68 us -> 80.1 us
  matrix products: 17.9 us -> 4.05 us
  between operations: 14.5 us -> 1.1 us
  starting transfers between devices: 56.8 us -> 61.3 us
  local copies, waits for them, and re-layouts: 3.76 us -> 6.95 us
    all_gather x2 -> x0, waiting for transfers between devices: 122 us -> none  [the longest x1 67.2 us: shards(): portion = lax.all_gather(tokens, 'head', axis=1, tiled=True)]
    pallas_call x0 -> x2, Pallas kernels: none -> 71.4 us  [gather_matmul(): pl.pallas_call(functools.partial(gather_kernel, sizes=sizes), out_shape=[...]
    dot_general x3 -> x0, matrix products: 13.8 us -> none  [the longest x1 7.34 us: shards(): jnp.dot(portion, w_proj, precision=high, preferred_element_type=F32)]
    ppermute x11, waiting for transfers between devices: 10.6 us -> 4.14 us  [partner(): return lax.ppermute(value, axis, pairs)]
    ppermute x11, starting transfers between devices: 54 us -> 60.1 us  [partner(): return lax.ppermute(value, axis, pairs)]
    unnamed x16 -> x20, local copies, waits for them, and re-layouts: 2.85 us -> 6.04 us
  transfers between devices with their start and end apart: 14 -> 12, of which waited for: 5 -> 3; matrix products, arithmetic and copies ran while one was open for 3% -> 3% of each run, Pallas kernels for 0% -> 0%
where the time goes in v2:
time: 158 us
  Pallas kernels  80.1 us (51%)
  starting transfers between devices  61.3 us (39%)
  local copies, waits for them, and re-layouts  6.95 us (4%)
  waiting for transfers between devices  4.15 us (3%)
  matrix products  4.05 us (3%)
    pallas_call x2, Pallas kernels, gather_matmul(): pl.pallas_call(functools.partial(gather_kernel, sizes=sizes), out_shape=[...  71.4 us
    ppermute x11, starting transfers between devices, partner(): return lax.ppermute(value, axis, pairs)  60.1 us
    unnamed x20, local copies, waits for them, and re-layouts  6.04 us
    pallas_call x1, Pallas kernels, shards(): pl.pallas_call(block_kernel, out_shape=[jax.ShapeDtypeStruct((rows, DK),...  4.77 us
    ppermute x11, waiting for transfers between devices, partner(): return lax.ppermute(value, axis, pairs)  4.14 us
    pallas_call x1, Pallas kernels, shards(): pl.pallas_call(mix_kernel, out_shape=jax.ShapeDtypeStruct((rows, DK), F32...  3.9 us
  transfers between devices with their start and end apart: 12, of which 3 were waited for; matrix products, arithmetic and copies ran while one was open for 3% of the time, Pallas kernels for 0%

profile of v2, /device:TPU:1, one launch (start us, length us, event | category | flops | bytes accessed | tf_op | source)
XLA Modules:
  0.0 157.7 jit_solution(9553063272948637467)
XLA Ops:
  0.0 1.3 copy.10.refs_1_
  1.3 0.9 copy-done.5
  2.2 40.3 %project.1 = (f32[512,512]{1,0:T(8,128)S(1)}, f32[512,9]{1,0:T(8,128)S(1)}) custom-call(f32[512,128]{1,0:T(8,128)S(1)} %copy-done.5, f32[2048,512]{1,0:T(8,128)} %refs_0_.2, f32[2048,9]{1,0:T(8,128)S(1)} %copy.10.refs_1_), custom_call_target="tpu_custom_call" | custom-call | tf_op jit(solution)/shard_map/project/pallas_call | solution.py:295
  42.6 1.3 collective-permute-start
  44.7 4.8 %block.1 = (f32[512,128]{1,0:T(8,128)S(1)}, f32[512,128]{1,0:T(8,128)S(1)}, f32[256,128]{1,0:T(8,128)S(1)}, f32[512,9]{1,0:T(8,128)S(1)}) custom-call(f32[512,512]{1,0:T(8,128)S(1)} %get-tuple-element.11.proj_ref, f32[8,384]{1,0:T(8,128)S(1)} %collective-permute-done.prior_ref, f32[4,384]{1,0:T(4,128)S(1)} %copy-done.6, ...), custom_call_target="tpu_custom_call" | custom-call | tf_op jit(solution)/shard_map/block/pallas_call | solution.py:333
  49.5 0.7 copy-done.2
  50.2 0.7 copy-done.3
  51.0 3.6 %collective-permute-start.2 = (f32[128,128]{1,0:T(8,128)S(1)}, f32[128,128]{1,0:T(8,128)S(1)}, u32[]{:S(2)}, u32[]{:S(2)}) collective-permute-start(f32[128,128]{1,0:T(8,128)S(1)} %get-tuple-element.17), channel_id=1, source_target_pairs={{0,16},{16,0},{32,48},{48,32},{64,80},{80,64},{96,112},{112,96},{1... | collective-permute-start | bytes 196616 | tf_op jit(solution)/shard_map/ppermute | solution.py:325
  54.6 0.8 slice.15.gate_ref
  55.3 1.9 %collective-permute-start.1 = (f32[128,128]{1,0:T(8,128)S(1)}, f32[128,128]{1,0:T(8,128)S(1)}, u32[]{:S(2)}, u32[]{:S(2)}) collective-permute-start(f32[128,128]{1,0:T(8,128)S(1)} %get-tuple-element.18), channel_id=1, source_target_pairs={{0,16},{16,0},{32,48},{48,32},{64,80},{80,64},{96,112},{112,96},{1... | collective-permute-start | bytes 196616 | tf_op jit(solution)/shard_map/ppermute | solution.py:325
  57.4 1.9 %collective-permute-start.4 = (f32[128,128]{1,0:T(8,128)S(1)}, f32[128,128]{1,0:T(8,128)S(1)}, u32[]{:S(2)}, u32[]{:S(2)}) collective-permute-start(f32[128,128]{1,0:T(8,128)S(1)} %fusion.19), channel_id=1, source_target_pairs={{0,32},{16,48},{32,0},{48,16},{64,96},{80,112},{96,64},{112,80},{1... | collective-permute-start | bytes 196616 | tf_op jit(solution)/shard_map/ppermute | solution.py:325
  59.4 0.9 collective-permute-done.1
  60.3 0.2 convolution_add_fusion.4
  60.5 3.3 %collective-permute-start.3 = (f32[128,128]{1,0:T(8,128)S(1)}, f32[128,128]{1,0:T(8,128)S(1)}, u32[]{:S(2)}, u32[]{:S(2)}) collective-permute-start(f32[128,128]{1,0:T(8,128)S(1)} %convolution_add_fusion.4), channel_id=1, source_target_pairs={{0,32},{16,48},{32,0},{48,16},{64,96},{80,112},{96,64},{112,80},{1... | collective-permute-start | bytes 196616 | tf_op jit(solution)/shard_map/ppermute | solution.py:325
  64.3 0.2 fusion.15
  64.5 8.3 %collective-permute-start.6 = (f32[128,128]{1,0:T(8,128)S(1)}, f32[128,128]{1,0:T(8,128)S(1)}, u32[]{:S(2)}, u32[]{:S(2)}) collective-permute-start(f32[128,128]{1,0:T(8,128)S(1)} %fusion.15), channel_id=1, source_target_pairs={{0,64},{16,80},{32,96},{48,112},{64,0},{80,16},{96,32},{112,48},{1... | collective-permute-start | bytes 196616 | tf_op jit(solution)/shard_map/ppermute | solution.py:325
  72.8 0.2 convolution_add_fusion.3
  73.0 2.5 %collective-permute-start.5 = (f32[128,128]{1,0:T(8,128)S(1)}, f32[128,128]{1,0:T(8,128)S(1)}, u32[]{:S(2)}, u32[]{:S(2)}) collective-permute-start(f32[128,128]{1,0:T(8,128)S(1)} %convolution_add_fusion.3), channel_id=1, source_target_pairs={{0,64},{16,80},{32,96},{48,112},{64,0},{80,16},{96,32},{112,48},{1... | collective-permute-start | bytes 196616 | tf_op jit(solution)/shard_map/ppermute | solution.py:325
  76.1 12.6 %collective-permute-start.8 = (f32[128,128]{1,0:T(8,128)S(1)}, f32[128,128]{1,0:T(8,128)S(1)}, u32[]{:S(2)}, u32[]{:S(2)}) collective-permute-start(f32[128,128]{1,0:T(8,128)S(1)} %fusion.11), channel_id=1, source_target_pairs={{0,128},{16,144},{32,160},{48,176},{64,192},{80,208},{96,224},{112... | collective-permute-start | bytes 196616 | tf_op jit(solution)/shard_map/ppermute | solution.py:325
  88.7 0.2 convolution_add_fusion.2
  89.0 6.4 %collective-permute-start.7 = (f32[128,128]{1,0:T(8,128)S(1)}, f32[128,128]{1,0:T(8,128)S(1)}, u32[]{:S(2)}, u32[]{:S(2)}) collective-permute-start(f32[128,128]{1,0:T(8,128)S(1)} %convolution_add_fusion.2), channel_id=1, source_target_pairs={{0,128},{16,144},{32,160},{48,176},{64,192},{80,208},{96,224},{112... | collective-permute-start | bytes 196616 | tf_op jit(solution)/shard_map/ppermute | solution.py:325
  96.0 12.0 %collective-permute-start.10 = (f32[128,128]{1,0:T(8,128)S(1)}, f32[128,128]{1,0:T(8,128)S(1)}, u32[]{:S(2)}, u32[]{:S(2)}) collective-permute-start(f32[128,128]{1,0:T(8,128)S(1)} %fusion.7), channel_id=1, source_target_pairs={{0,256},{16,272},{32,288},{48,304},{64,320},{80,336},{96,352},{112... | collective-permute-start | bytes 196616 | tf_op jit(solution)/shard_map/ppermute | solution.py:325
  108.1 0.2 convolution_add_fusion.1
  108.3 2.8 %collective-permute-start.9 = (f32[128,128]{1,0:T(8,128)S(1)}, f32[128,128]{1,0:T(8,128)S(1)}, u32[]{:S(2)}, u32[]{:S(2)}) collective-permute-start(f32[128,128]{1,0:T(8,128)S(1)} %convolution_add_fusion.1), channel_id=1, source_target_pairs={{0,256},{16,272},{32,288},{48,304},{64,320},{80,336},{96,352},{112... | collective-permute-start | bytes 196616 | tf_op jit(solution)/shard_map/ppermute | solution.py:325
  111.6 1.8 %collective-permute-done.9 = f32[128,128]{1,0:T(8,128)S(1)} collective-permute-done((f32[128,128]{1,0:T(8,128)S(1)}, f32[128,128]{1,0:T(8,128)S(1)}, u32[]{:S(2)}, u32[]{:S(2)}) %collective-permute-start.9) | collective-permute-done | bytes 65568 | tf_op jit(solution)/shard_map/ppermute | solution.py:325
  113.5 4.6 %collective-permute-start.11 = (f32[128,128]{1,0:T(8,128)S(1)}, f32[128,128]{1,0:T(8,128)S(1)}, u32[]{:S(2)}, u32[]{:S(2)}) collective-permute-start(f32[128,128]{1,0:T(8,128)S(1)} %convolution_add_fusion), channel_id=1, source_target_pairs={{0,512},{16,528},{32,544},{48,560},{64,576},{80,592},{96,608},{112... | collective-permute-start | bytes 196616 | tf_op jit(solution)/shard_map/ppermute | solution.py:325
  118.6 1.4 collective-permute-done.11
  120.3 0.7 copy-done.7
  121.0 3.9 %mix.1.x_ref = f32[512,128]{1,0:T(8,128)} custom-call(f32[512,128]{1,0:T(8,128)} %copy-done.2, f32[512,128]{1,0:T(8,128)} %copy-done.3, f32[512,9]{1,0:T(8,128)} %copy-done.4, f32[768,128]{1,0:T(8,128)} %copy-done.7, f32[512,128]{1,0:T(8,128)} %slice.15.gate_ref, f32[1,128]{1,0:T(1,128)} %bitcast.12), custom_call_target="tpu_custom_call" | custom-call | tf_op jit(solution)/shard_map/mix/pallas_call | solution.py:366
  124.9 0.9 copy-done.1
  125.9 31.1 %combine.1 = f32[512,128]{1,0:T(8,128)S(1)} custom-call(f32[512,128]{1,0:T(8,128)S(1)} %copy-done.1, f32[2048,128]{1,0:T(8,128)S(1)} %copy-done), custom_call_target="tpu_custom_call" | custom-call | tf_op jit(solution)/shard_map/combine/pallas_call | solution.py:295
  157.0 0.7 copy.19
  (41 shorter events, 3.2 us)
Async XLA Ops:
  0.0 44.5 %copy-start.8 = (s32[512]{0:T(512)S(1)}, s32[512]{0:T(512)}, u32[]{:S(2)}) copy-start(s32[512]{0:T(512)} %param.13) | copy-start | bytes 6148
  0.0 44.7 %copy-start.6 = (f32[4,384]{1,0:T(4,128)S(1)}, f32[4,384]{1,0:T(4,128)}, u32[]{:S(2)}) copy-start(f32[4,384]{1,0:T(4,128)} %conv_ref.1) | copy-start | bytes 18436
  1.3 1.0 copy-start.5
  42.6 2.1 %collective-permute-start = (f32[8,384]{1,0:T(8,128)S(1)}, f32[8,384]{1,0:T(8,128)S(1)}, u32[]{:S(2)}, u32[]{:S(2)}) collective-permute-start(f32[8,384]{1,0:T(8,128)S(1)} %slice.12), channel_id=1, source_target_pairs={{0,16},{16,32},{32,48},{48,64},{64,80},{80,96},{96,112},{112,128},... | collective-permute-start | bytes 36872 | tf_op jit(solution)/shard_map/ppermute | solution.py:319
  44.7 80.2 %copy-start = (f32[2048,128]{1,0:T(8,128)S(1)}, f32[2048,128]{1,0:T(8,128)}, u32[]{:S(2)}) copy-start(f32[2048,128]{1,0:T(8,128)} %refs_0_.3) | copy-start | bytes 3145732
  49.5 0.7 copy-start.2
  50.2 0.7 copy-start.3
  50.9 69.3 %copy-start.4 = (f32[512,9]{1,0:T(8,128)}, f32[512,9]{1,0:T(8,128)S(1)}, u32[]{:S(2)}) copy-start(f32[512,9]{1,0:T(8,128)S(1)} %get-tuple-element.15.weights_ref) | copy-start | bytes 55300
  51.0 6.3 %collective-permute-start.2 = (f32[128,128]{1,0:T(8,128)S(1)}, f32[128,128]{1,0:T(8,128)S(1)}, u32[]{:S(2)}, u32[]{:S(2)}) collective-permute-start(f32[128,128]{1,0:T(8,128)S(1)} %get-tuple-element.17), channel_id=1, source_target_pairs={{0,16},{16,0},{32,48},{48,32},{64,80},{80,64},{96,112},{112,96},{1... | collective-permute-start | bytes 196616 | tf_op jit(solution)/shard_map/ppermute | solution.py:325
  55.3 5.0 %collective-permute-start.1 = (f32[128,128]{1,0:T(8,128)S(1)}, f32[128,128]{1,0:T(8,128)S(1)}, u32[]{:S(2)}, u32[]{:S(2)}) collective-permute-start(f32[128,128]{1,0:T(8,128)S(1)} %get-tuple-element.18), channel_id=1, source_target_pairs={{0,16},{16,0},{32,48},{48,32},{64,80},{80,64},{96,112},{112,96},{1... | collective-permute-start | bytes 196616 | tf_op jit(solution)/shard_map/ppermute | solution.py:325
  57.4 6.8 %collective-permute-start.4 = (f32[128,128]{1,0:T(8,128)S(1)}, f32[128,128]{1,0:T(8,128)S(1)}, u32[]{:S(2)}, u32[]{:S(2)}) collective-permute-start(f32[128,128]{1,0:T(8,128)S(1)} %fusion.19), channel_id=1, source_target_pairs={{0,32},{16,48},{32,0},{48,16},{64,96},{80,112},{96,64},{112,80},{1... | collective-permute-start | bytes 196616 | tf_op jit(solution)/shard_map/ppermute | solution.py:325
  60.5 12.2 %collective-permute-start.3 = (f32[128,128]{1,0:T(8,128)S(1)}, f32[128,128]{1,0:T(8,128)S(1)}, u32[]{:S(2)}, u32[]{:S(2)}) collective-permute-start(f32[128,128]{1,0:T(8,128)S(1)} %convolution_add_fusion.4), channel_id=1, source_target_pairs={{0,32},{16,48},{32,0},{48,16},{64,96},{80,112},{96,64},{112,80},{1... | collective-permute-start | bytes 196616 | tf_op jit(solution)/shard_map/ppermute | solution.py:325
  64.5 11.4 %collective-permute-start.6 = (f32[128,128]{1,0:T(8,128)S(1)}, f32[128,128]{1,0:T(8,128)S(1)}, u32[]{:S(2)}, u32[]{:S(2)}) collective-permute-start(f32[128,128]{1,0:T(8,128)S(1)} %fusion.15), channel_id=1, source_target_pairs={{0,64},{16,80},{32,96},{48,112},{64,0},{80,16},{96,32},{112,48},{1... | collective-permute-start | bytes 196616 | tf_op jit(solution)/shard_map/ppermute | solution.py:325
  73.0 15.8 %collective-permute-start.5 = (f32[128,128]{1,0:T(8,128)S(1)}, f32[128,128]{1,0:T(8,128)S(1)}, u32[]{:S(2)}, u32[]{:S(2)}) collective-permute-start(f32[128,128]{1,0:T(8,128)S(1)} %convolution_add_fusion.3), channel_id=1, source_target_pairs={{0,64},{16,80},{32,96},{48,112},{64,0},{80,16},{96,32},{112,48},{1... | collective-permute-start | bytes 196616 | tf_op jit(solution)/shard_map/ppermute | solution.py:325
  76.1 19.7 %collective-permute-start.8 = (f32[128,128]{1,0:T(8,128)S(1)}, f32[128,128]{1,0:T(8,128)S(1)}, u32[]{:S(2)}, u32[]{:S(2)}) collective-permute-start(f32[128,128]{1,0:T(8,128)S(1)} %fusion.11), channel_id=1, source_target_pairs={{0,128},{16,144},{32,160},{48,176},{64,192},{80,208},{96,224},{112... | collective-permute-start | bytes 196616 | tf_op jit(solution)/shard_map/ppermute | solution.py:325
  89.0 19.1 %collective-permute-start.7 = (f32[128,128]{1,0:T(8,128)S(1)}, f32[128,128]{1,0:T(8,128)S(1)}, u32[]{:S(2)}, u32[]{:S(2)}) collective-permute-start(f32[128,128]{1,0:T(8,128)S(1)} %convolution_add_fusion.2), channel_id=1, source_target_pairs={{0,128},{16,144},{32,160},{48,176},{64,192},{80,208},{96,224},{112... | collective-permute-start | bytes 196616 | tf_op jit(solution)/shard_map/ppermute | solution.py:325
  96.0 15.5 %collective-permute-start.10 = (f32[128,128]{1,0:T(8,128)S(1)}, f32[128,128]{1,0:T(8,128)S(1)}, u32[]{:S(2)}, u32[]{:S(2)}) collective-permute-start(f32[128,128]{1,0:T(8,128)S(1)} %fusion.7), channel_id=1, source_target_pairs={{0,256},{16,272},{32,288},{48,304},{64,320},{80,336},{96,352},{112... | collective-permute-start | bytes 196616 | tf_op jit(solution)/shard_map/ppermute | solution.py:325
  108.3 5.0 %collective-permute-start.9 = (f32[128,128]{1,0:T(8,128)S(1)}, f32[128,128]{1,0:T(8,128)S(1)}, u32[]{:S(2)}, u32[]{:S(2)}) collective-permute-start(f32[128,128]{1,0:T(8,128)S(1)} %convolution_add_fusion.1), channel_id=1, source_target_pairs={{0,256},{16,272},{32,288},{48,304},{64,320},{80,336},{96,352},{112... | collective-permute-start | bytes 196616 | tf_op jit(solution)/shard_map/ppermute | solution.py:325
  113.5 6.5 %collective-permute-start.11 = (f32[128,128]{1,0:T(8,128)S(1)}, f32[128,128]{1,0:T(8,128)S(1)}, u32[]{:S(2)}, u32[]{:S(2)}) collective-permute-start(f32[128,128]{1,0:T(8,128)S(1)} %convolution_add_fusion), channel_id=1, source_target_pairs={{0,512},{16,528},{32,544},{48,560},{64,576},{80,592},{96,608},{112... | collective-permute-start | bytes 196616 | tf_op jit(solution)/shard_map/ppermute | solution.py:325
  120.3 0.7 copy-start.7
  124.9 1.0 copy-start.1

commit v3 on v2

--- a/solution.py
+++ b/solution.py
@@ -136,21 +136,6 @@
     pair_ref[...] = state
 
 
-def mix_kernel(carried_ref, local_ref, weights_ref, states_ref, gate_ref, gain_ref, out_ref):
-    levels = states_ref.shape[0] // DK
-    rows = carried_ref.shape[0]
-    for base in range(0, rows, CHUNK):
-        weights = weights_ref[base:base + CHUNK]
-        mixed = weights[:, 2:3] * local_ref[base:base + CHUNK]
-        carried = left(carried_ref[base:base + CHUNK])
-        for level in range(levels):
-            state = states_ref[level * DK:(level + 1) * DK].T
-            mixed = mixed + weights[:, level + 3:level + 4] * product(carried, right(state))
-        scale = lax.rsqrt(jnp.mean(mixed * mixed, axis=1, keepdims=True) + 1e-05)
-        gate = gate_ref[base:base + CHUNK]
-        out_ref[base:base + CHUNK] = mixed * scale * gain_ref[...] * (gate * jax.nn.sigmoid(gate))
-
-
 PARTS = 4
 
 
@@ -313,20 +298,187 @@
     )(values, *weights)
 
 
+NZ = 16
+RING_PARTS = 4
+
+
+class Ring:
+    def __init__(self, place, n, targets, source, held, send_sem, recv_sem, parts=RING_PARTS):
+        self.place, self.n, self.targets, self.source, self.held = place, n, targets, source, held
+        self.send_sem, self.recv_sem, self.parts = send_sem, recv_sem, parts
+        self.half = n // 2
+        self.part = source.shape[0] // parts
+
+    def goes(self, direction, hop, index):
+        longest = self.half if (index < self.parts // 2) == (direction == 0) else self.half - 1
+        return hop <= longest
+
+    def copy(self, direction, hop, index, first=False):
+        span = pl.ds(index * self.part, self.part)
+        offset = self.n - hop if direction == 0 else hop
+        slot = self.place if first else lax.rem(self.place + offset, self.n)
+        source = self.source if first else self.held.at[slot]
+        return pltpu.make_async_remote_copy(
+            src_ref=source.at[span],
+            dst_ref=self.held.at[slot, span],
+            send_sem=self.send_sem.at[direction, hop, index],
+            recv_sem=self.recv_sem.at[direction, hop, index],
+            device_id=self.targets[direction],
+            device_id_type=MESH,
+        )
+
+    def begin(self):
+        for index in range(self.parts):
+            for direction in range(2):
+                if self.goes(direction, 1, index):
+                    self.copy(direction, 0, index, True).start()
+        self.held[self.place] = self.source[...]
+
+    def arrive(self, hop):
+        for index in range(self.parts):
+            for direction in range(2):
+                @pl.when(self.goes(direction, hop, index))
+                def _():
+                    self.copy(direction, hop - 1, index).wait_recv()
+
+                @pl.when(self.goes(direction, hop + 1, index))
+                def _():
+                    self.copy(direction, hop, index).start()
+
+    def run(self):
+        def step(hop, carry):
+            self.arrive(hop)
+            return carry
+
+        lax.fori_loop(1, self.half + 1, step, 0)
+
+    def end(self):
+        for index in range(self.parts):
+            for direction in range(2):
+                for hop in range(self.half):
+                    if self.goes(direction, hop + 1, index):
+                        self.copy(direction, hop, index, True).wait_send()
+
+
+def join(first, second):
+    moved = product(left(first), right(second[:DK]))
+    return jnp.concatenate([moved[:DK], moved[DK:] + second[DK:]], axis=0)
+
+
+def reduce_ring(held, tree, count, last):
+    nodes = [held[index] for index in range(count)]
+    level = 0
+    while len(nodes) > (1 if last else 2):
+        nodes = [join(nodes[2 * index], nodes[2 * index + 1]) for index in range(len(nodes) // 2)]
+        if len(nodes) > 1:
+            for index, node in enumerate(nodes):
+                tree[level, index] = node
+        level += 1
+    return nodes[0]
+
+
+def level_states(held, tree, count, place, carry, neutral):
+    states = []
+    for level in range(count.bit_length() - 1):
+        upper = (place >> level) & 1 == 1
+        index = jnp.maximum((place >> level) - 1, 0)
+        node = held[index] if level == 0 else tree[level - 1, index]
+        moved = product(left(jnp.where(upper, node, neutral)), right(carry))
+        carry = moved[:DK]
+        states.append(moved[DK:])
+    return states, carry
+
+
+def context_kernel(pair_ref, carried_ref, local_ref, weights_ref, gate_ref, gain_ref, out_ref,
+                   held_z, tree_z, held_x, tree_x, group_ref, mixed_ref,
+                   send_z, recv_z, send_x, recv_x):
+    count_z, count_x = held_z.shape[0], held_x.shape[0]
+    rows = carried_ref.shape[0]
+    me = lax.axis_index("ctx")
+    place_x, place_z = me // count_z, lax.rem(me, count_z)
+    targets_z = [
+        {"ctx": place_x * count_z + lax.rem(place_z + offset, count_z)} for offset in (1, count_z - 1)
+    ]
+    targets_x = [
+        {"ctx": lax.rem(place_x + offset, count_x) * count_z + place_z} for offset in (1, count_x - 1)
+    ]
+    barrier = pltpu.get_barrier_semaphore()
+    for neighbour in targets_z + targets_x:
+        pl.semaphore_signal(barrier, inc=1, device_id=neighbour, device_id_type=MESH)
+    pl.semaphore_wait(barrier, 4)
+
+    ring_z = Ring(place_z, count_z, targets_z, pair_ref, held_z, send_z, recv_z)
+    ring_x = Ring(place_x, count_x, targets_x, group_ref, held_x, send_x, recv_x)
+    ring_z.begin()
+    ring_z.run()
+    group_ref[...] = reduce_ring(held_z, tree_z, count_z, True)
+    ring_x.begin()
+
+    row_ids = lax.broadcasted_iota(jnp.int32, (2 * DK, DK), 0)
+    col_ids = lax.broadcasted_iota(jnp.int32, (2 * DK, DK), 1)
+    neutral = (row_ids == col_ids).astype(F32)
+    states, carry = level_states(held_z, tree_z, count_z, place_z, neutral[:DK], neutral)
+    done = len(states)
+
+    def mix(base, total, states, first):
+        carried = left(carried_ref[base:base + CHUNK])
+        for number, state in enumerate(states):
+            column = first + number
+            weight = weights_ref[base:base + CHUNK, column:column + 1]
+            total = total + weight * product(carried, state)
+        return total
+
+    turned = [right(state.T) for state in states]
+    for base in range(0, rows, CHUNK):
+        start = weights_ref[base:base + CHUNK, 2:3] * local_ref[base:base + CHUNK]
+        mixed_ref[base:base + CHUNK] = mix(base, start, turned, 3)
+    ring_x.run()
+    reduce_ring(held_x, tree_x, count_x, False)
+    states, carry = level_states(held_x, tree_x, count_x, place_x, carry, neutral)
+    turned = [right(state.T) for state in states]
+    for base in range(0, rows, CHUNK):
+        mixed = mix(base, mixed_ref[base:base + CHUNK], turned, 3 + done)
+        scale = lax.rsqrt(jnp.mean(mixed * mixed, axis=1, keepdims=True) + 1e-05)
+        gate = gate_ref[base:base + CHUNK]
+        out_ref[base:base + CHUNK] = mixed * scale * gain_ref[...] * (gate * jax.nn.sigmoid(gate))
+    ring_z.end()
+    ring_x.end()
+
+
+def across_context(pair, carried, local, weights, projected, gain):
+    rows = carried.shape[0]
+    count = lax.axis_size("ctx")
+    count_z = min(NZ, count)
+    count_x = count // count_z
+    return pl.pallas_call(
+        context_kernel,
+        out_shape=jax.ShapeDtypeStruct((rows, DK), F32),
+        grid=(1,),
+        in_specs=[VMEM] * 4 + [pl.BlockSpec((rows, DK), lambda step: (0, 3)), VMEM],
+        out_specs=VMEM,
+        scratch_shapes=[
+            pltpu.VMEM((count_z, 2 * DK, DK), F32),
+            pltpu.VMEM((count_z.bit_length() - 2, count_z // 2, 2 * DK, DK), F32),
+            pltpu.VMEM((count_x, 2 * DK, DK), F32),
+            pltpu.VMEM((max(count_x.bit_length() - 2, 1), count_x // 2, 2 * DK, DK), F32),
+            pltpu.VMEM((2 * DK, DK), F32),
+            pltpu.VMEM((rows, DK), F32),
+        ] + [pltpu.SemaphoreType.DMA((2, count_z // 2, RING_PARTS))] * 2
+          + [pltpu.SemaphoreType.DMA((2, count_x // 2, RING_PARTS))] * 2,
+        compiler_params=pltpu.CompilerParams(
+            collective_id=2, has_side_effects=True, vmem_limit_bytes=48 << 20
+        ),
+        name="context",
+    )(pair, carried, local, weights, projected, gain)
+
+
 def shifted(value, axis, steps):
     count = lax.axis_size(axis)
     initial, last = (max(0, -steps), min(count, count - steps))
     return lax.ppermute(value, axis, [(source, source + steps) for source in range(initial, last)])
 
 
-def partner(value, axis, bit):
-    mask = 2**bit
-    pairs = [(source, source ^ mask) for source in range(lax.axis_size(axis))]
-    return lax.ppermute(value, axis, pairs)
-
-
 def shards(tokens, w_proj, w_mix, conv_w, rates, doc_start, norm_gain, w_out):
-    highest = lax.Precision.HIGHEST
     rows = tokens.shape[0]
     projected, mixing = gather_matmul(tokens, [w_proj, w_mix], 0, "project")
     prior = shifted(projected[rows - RIM:, :3 * DK], "ctx", 1)
@@ -344,33 +496,7 @@
         compiler_params=pltpu.CompilerParams(vmem_limit_bytes=48 << 20),
         name="block",
     )(projected, prior, conv_w, mixing, doc_start.astype(F32)[:, None], rates)
-    my_index = lax.axis_index("ctx")
-    nbits = lax.axis_size("ctx").bit_length() - 1
-    group_a, group_b = pair[:DK], pair[DK:]
-    identity_d = jnp.eye(DK, dtype=F32)
-    carry_m = identity_d
-    level_states = []
-    for level in range(nbits):
-        other_a, other_b = partner((group_a, group_b), "ctx", level)
-        upper = my_index >> level & 1 == 1
-        seg_a = jnp.where(upper, other_a, identity_d)
-        seg_b = jnp.where(upper, other_b, 0.0)
-        first_a = jnp.where(upper, other_a, group_a)
-        first_b = jnp.where(upper, other_b, group_b)
-        second_a = jnp.where(upper, group_a, other_a)
-        second_b = jnp.where(upper, group_b, other_b)
-        group_a = jnp.dot(first_a, second_a, precision=highest, preferred_element_type=F32)
-        group_b = jnp.dot(first_b, second_a, precision=highest, preferred_element_type=F32) + second_b
-        level_states.append(jnp.dot(seg_b, carry_m, precision=highest, preferred_element_type=F32))
-        carry_m = jnp.dot(seg_a, carry_m, precision=highest, preferred_element_type=F32)
-    normed = pl.pallas_call(
-        mix_kernel,
-        out_shape=jax.ShapeDtypeStruct((rows, DK), F32),
-        in_specs=[VMEM] * 6,
-        out_specs=VMEM,
-        name="mix",
-    )(carried, local, weights, jnp.concatenate(level_states, axis=0), projected[:, 3 * DK:],
-      norm_gain[None, :])
+    normed = across_context(pair, carried, local, weights, projected, norm_gain[None, :])
     return gather_matmul(normed, [w_out], 1, "combine")[0]
 
 

time: 158 us -> 129 us (0.82)
  starting transfers between devices: 61.3 us -> 1.29 us
  Pallas kernels: 80.1 us -> 123 us
  waiting for transfers between devices: 4.15 us -> 0.01 us
  matrix products: 4.05 us -> 0 us
  local copies, waits for them, and re-layouts: 6.95 us -> 3.1 us
    ppermute x11 -> x0, starting transfers between devices: 60.1 us -> none  [partner(): return lax.ppermute(value, axis, pairs)]
    pallas_call x1, Pallas kernels: 3.9 us -> 43.8 us  [across_context(): pl.pallas_call(context_kernel, out_shape=jax.ShapeDtypeStruct((rows, DK),...]
    ppermute x11 -> x0, waiting for transfers between devices: 4.14 us -> none  [partner(): return lax.ppermute(value, axis, pairs)]
    dot_general x20 -> x0, matrix products: 4.05 us -> none  [the longest x6 1.2 us: shards(): jnp.dot(seg_b, carry_m, precision=highest, preferred_element_type=F32)]
    pallas_call x2, Pallas kernels: 71.4 us -> 74.7 us  [gather_matmul(): pl.pallas_call(functools.partial(gather_kernel, sizes=sizes), out_shape=[...]
    unnamed x20 -> x12, local copies, waits for them, and re-layouts: 6.04 us -> 2.96 us
  transfers between devices with their start and end apart: 12 -> 1, of which waited for: 3 -> 0; matrix products, arithmetic and copies ran while one was open for 3% -> 0% of each run, Pallas kernels for 0% -> 0%
where the time goes in v3:
time: 129 us; the launch traced here: 128 us
  Pallas kernels  123 us (95%)
  local copies, waits for them, and re-layouts  3.1 us (2%)
  starting transfers between devices  1.29 us (1%)
    pallas_call x2, Pallas kernels, gather_matmul(): pl.pallas_call(functools.partial(gather_kernel, sizes=sizes), out_shape=[...  74.7 us
    pallas_call x1, Pallas kernels, across_context(): pl.pallas_call(context_kernel, out_shape=jax.ShapeDtypeStruct((rows, DK),...  43.8 us
    pallas_call x1, Pallas kernels, shards(): pl.pallas_call(block_kernel, out_shape=[jax.ShapeDtypeStruct((rows, DK),...  4.77 us
    unnamed x12, local copies, waits for them, and re-layouts  2.96 us
  transfers between devices with their start and end apart: 1, of which 0 were waited for; matrix products, arithmetic and copies ran while one was open for 0% of the time, Pallas kernels for 0%

profile of v3, /device:TPU:1, one launch (start us, length us, event | category | flops | bytes accessed | tf_op | source)
XLA Modules:
  0.0 128.4 jit_solution(9716987085603340939)
XLA Ops:
  0.0 0.0 copy-start.4
  0.0 0.0 copy-start.2
  0.0 0.0 copy-start.3
  0.0 1.3 %copy.10.refs_1_ = f32[2048,9]{1,0:T(8,128)S(1)} copy(f32[2048,9]{0,1:T(8,128)} %param.10) | data formatting | bytes 147456 | tf_op args[2]
  1.3 0.0 copy-start.1
  1.3 0.9 copy-done.1
  2.3 0.0 copy-start
  2.3 40.5 %project.1 = (f32[512,512]{1,0:T(8,128)S(1)}, f32[512,9]{1,0:T(8,128)S(1)}) custom-call(f32[512,128]{1,0:T(8,128)S(1)} %copy-done.1, f32[2048,512]{1,0:T(8,128)} %refs_0_.2, f32[2048,9]{1,0:T(8,128)S(1)} %copy.10.refs_1_), custom_call_target="tpu_custom_call" | custom-call | tf_op jit(solution)/shard_map/project/pallas_call | solution.py:280
  42.7 1.3 %collective-permute-start = (f32[8,384]{1,0:T(8,128)S(1)}, f32[8,384]{1,0:T(8,128)S(1)}, u32[]{:S(2)}, u32[]{:S(2)}) collective-permute-start(f32[8,384]{1,0:T(8,128)S(1)} %slice.3), channel_id=1, source_target_pairs={{0,16},{16,32},{32,48},{48,64},{64,80},{80,96},{96,112},{112,128},... | collective-permute-start | bytes 36872 | tf_op jit(solution)/shard_map/ppermute | solution.py:478
  44.0 0.0 copy-done.4
  44.1 0.1 copy.11.doc_ref
  44.9 0.0 collective-permute-done.prior_ref
  44.9 0.0 copy-done.2
  44.9 4.8 %block.1 = (f32[512,128]{1,0:T(8,128)S(1)}, f32[512,128]{1,0:T(8,128)S(1)}, f32[256,128]{1,0:T(8,128)S(1)}, f32[512,9]{1,0:T(8,128)S(1)}) custom-call(f32[512,512]{1,0:T(8,128)S(1)} %get-tuple-element.11.proj_ref.gate_ref, f32[8,384]{1,0:T(8,128)S(1)} %collective-permute-done.prior_ref, f32[4,384]{1,0:T(4,128)S(1)} %copy-done.2, ...), custom_call_target="tpu_custom_call" | custom-call | tf_op jit(solution)/shard_map/block/pallas_call | solution.py:485
  49.7 0.0 copy-done.3
  49.7 43.8 %context.1.x_ref = f32[512,128]{1,0:T(8,128)S(1)} custom-call(f32[256,128]{1,0:T(8,128)S(1)} %get-tuple-element.13.pair_ref, f32[512,128]{1,0:T(8,128)S(1)} %get-tuple-element.14.carried_ref, f32[512,128]{1,0:T(8,128)S(1)} %get-tuple-element.15.local_ref, f32[512,9]{1,0:T(8,128)S(1)} %get-tuple-element.16.weights_ref, ...), custom_call_target="tpu_custom_call" | custom-call | tf_op jit(solution)/shard_map/context/pallas_call | solution.py:453
  93.5 0.0 copy-done
  93.5 34.2 %combine.1 = f32[512,128]{1,0:T(8,128)S(1)} custom-call(f32[512,128]{1,0:T(8,128)S(1)} %context.1.x_ref, f32[2048,128]{1,0:T(8,128)S(1)} %copy-done), custom_call_target="tpu_custom_call" | custom-call | tf_op jit(solution)/shard_map/combine/pallas_call | solution.py:280
  127.7 0.7 copy.14
  (2 shorter events, 0.0 us)
Async XLA Ops:
  0.0 44.0 %copy-start.4 = (s32[512]{0:T(512)S(1)}, s32[512]{0:T(512)}, u32[]{:S(2)}) copy-start(s32[512]{0:T(512)} %param.13) | copy-start | bytes 6148
  0.0 44.9 %copy-start.2 = (f32[4,384]{1,0:T(4,128)S(1)}, f32[4,384]{1,0:T(4,128)}, u32[]{:S(2)}) copy-start(f32[4,384]{1,0:T(4,128)} %conv_ref.1) | copy-start | bytes 18436
  0.0 49.7 %copy-start.3 = (f32[128]{0:T(128)S(1)}, f32[128]{0:T(128)}, u32[]{:S(2)}) copy-start(f32[128]{0:T(128)} %param.14) | copy-start | bytes 1540
  1.3 1.0 copy-start.1
  2.3 91.3 %copy-start = (f32[2048,128]{1,0:T(8,128)S(1)}, f32[2048,128]{1,0:T(8,128)}, u32[]{:S(2)}) copy-start(f32[2048,128]{1,0:T(8,128)} %refs_0_.3) | copy-start | bytes 3145732
  42.7 2.1 %collective-permute-start = (f32[8,384]{1,0:T(8,128)S(1)}, f32[8,384]{1,0:T(8,128)S(1)}, u32[]{:S(2)}, u32[]{:S(2)}) collective-permute-start(f32[8,384]{1,0:T(8,128)S(1)} %slice.3), channel_id=1, source_target_pairs={{0,16},{16,32},{32,48},{48,64},{64,80},{80,96},{96,112},{112,128},... | collective-permute-start | bytes 36872 | tf_op jit(solution)/shard_map/ppermute | solution.py:478

commit v4 on v1

v4 whole, which is shorter than its diff:
```python
import jax
import jax.numpy as jnp
from jax import lax
from jax.experimental import pallas as pl
from jax.experimental.pallas import tpu as pltpu
from jax.sharding import PartitionSpec as P

F32 = jnp.float32
BF16 = jnp.bfloat16
DK = 128
CHUNK = 128
RIM = 8
NZ = 16
PARTS = 4
MESH = pl.DeviceIdType.MESH
VMEM = pl.BlockSpec(memory_space=pltpu.VMEM)
SMEM = pl.BlockSpec(memory_space=pltpu.SMEM)
ANY = pl.BlockSpec(memory_space=pl.ANY)


def split(value):
    high = value.astype(BF16)
    return high, (value - high.astype(F32)).astype(BF16)


def left(value):
    high, low = split(value)
    return jnp.concatenate([high, low], axis=1)


def right(value):
    high, low = split(value)
    both = jnp.concatenate([high, low], axis=1)
    return jnp.concatenate([both, both], axis=0)


def product(lhs, rhs):
    out = jnp.dot(lhs, rhs, preferred_element_type=F32)
    return out[:, :DK] + out[:, DK:]


def softplus(value):
    return jnp.maximum(value, 0.0) + jnp.log1p(jnp.exp(-jnp.abs(value)))


def join(first, second):
    moved = product(left(first), right(second[:DK]))
    return jnp.concatenate([moved[:DK], moved[DK:] + second[DK:]], axis=0)


class Ring:
    def __init__(self, place, n, targets, source, held, send_sem, recv_sem, stride=1, phase=0, pass_on=None):
        self.place, self.n, self.targets, self.source, self.held = place, n, targets, source, held
        self.send_sem, self.recv_sem, self.stride, self.phase = send_sem, recv_sem, stride, phase
        self.pass_on = pass_on
        self.half = n // 2
        self.part = source.shape[0] // PARTS

    def slot(self, place):
        return place * self.stride + self.phase

    def span(self, index):
        return pl.ds(index * self.part, self.part)

    def goes(self, direction, hop, index):
        longest = self.half if (index < PARTS // 2) == (direction == 0) else self.half - 1
        return hop <= longest

    def offset(self, direction, hop):
        return lax.rem(self.n - hop if direction == 0 else hop + 0, self.n)

    def copy(self, direction, hop, index, first=False):
        slot = self.slot(self.place if first else lax.rem(self.place + self.offset(direction, hop), self.n))
        source = self.source if first else self.held.at[slot]
        return pltpu.make_async_remote_copy(
            src_ref=source.at[self.span(index)],
            dst_ref=self.held.at[slot, self.span(index)],
            send_sem=self.send_sem.at[direction, hop, index],
            recv_sem=self.recv_sem.at[direction, hop, index],
            device_id=self.targets[direction],
            device_id_type=MESH,
        )

    def begin(self, index):
        for direction in range(2):
            if self.goes(direction, 1, index):
                self.copy(direction, 0, index, True).start()
        if self.pass_on is not None:
            self.pass_on(self.slot(self.place), 0, index, self.source).start()

    def arrive(self, hop, guard=True):
        for index in range(PARTS):
            for direction in range(2):
                here = guard & self.goes(direction, hop, index)

                @pl.when(here)
                def _():
                    self.copy(direction, hop - 1, index).wait_recv()

                @pl.when(guard & self.goes(direction, hop + 1, index))
                def _():
                    self.copy(direction, hop, index).start()

                if self.pass_on is not None:
                    @pl.when(here)
                    def _():
                        offset = self.offset(direction, hop)
                        slot = self.slot(lax.rem(self.place + offset, self.n))
                        self.pass_on(slot, offset, index, self.held.at[slot]).start()

    def run(self, first=1):
        def step(hop, carry):
            self.arrive(hop)
            return carry

        lax.fori_loop(first, self.half + 1, step, 0)

    def end(self):
        for index in range(PARTS):
            for direction in range(2):
                for hop in range(self.half):
                    if self.goes(direction, hop + 1, index):
                        self.copy(direction, hop, index, True).wait_send()
            if self.pass_on is not None:
                for offset in range(self.n):
                    self.pass_on(self.slot(self.place), offset, index, self.source).wait_send()


def multiply_arrivals(ring, multiply):
    def step(hop, carry):
        ring.arrive(hop, hop >= 1)

        def block(which, inner):
            offset = lax.rem(jnp.where(which == 0, hop, ring.n - hop), ring.n)
            there = lax.rem(ring.place + offset, ring.n)
            for index in range(PARTS):
                other = there * 2 + 1 - ring.phase
                ring.pass_on(other, offset, index, ring.held.at[other]).wait_recv()
            lhs = jnp.concatenate([ring.held[there * 2], ring.held[there * 2 + 1]], axis=1)
            multiply(split(lhs), pl.multiple_of(there * 2 * DK, 2 * DK))
            return inner

        lax.fori_loop(0, jnp.where((hop == 0) | (hop == ring.half), 1, 2), block, 0)
        return carry

    lax.fori_loop(0, ring.half + 1, step, 0)


def reduce_ring(held, tree, count, last):
    nodes = [held[index] for index in range(count)]
    level = 0
    while len(nodes) > (1 if last else 2):
        nodes = [join(nodes[2 * index], nodes[2 * index + 1]) for index in range(len(nodes) // 2)]
        if len(nodes) > 1:
            for index, node in enumerate(nodes):
                tree[level, index] = node
        level += 1
    return nodes[0]


def level_states(held, tree, count, place, carry, neutral):
    states = []
    for level in range(count.bit_length() - 1):
        upper = (place >> level) & 1 == 1
        index = jnp.maximum((place >> level) - 1, 0)
        node = held[index] if level == 0 else tree[level - 1, index]
        moved = product(left(jnp.where(upper, node, neutral)), right(carry))
        carry = moved[:DK]
        states.append(moved[DK:])
    return states, carry


def layer(tokens_ref, w_proj_ref, w_mix_ref, conv_ref, rate_ref, doc_ref, gain_ref, w_out_ref, out_ref,
          held_in, held_out, w_proj, w_out, raw_ref, mixing_ref, padded_ref, prior_ref,
          pair_ref, held_z, tree_z, group_ref, held_x, tree_x, local_ref, carried_ref, normed_ref,
          load_sem, rim_sem, send_y, recv_y, near_send, near_recv,
          send_z, recv_z, send_x, recv_x):
    rows = tokens_ref.shape[0]
    chunks = rows // CHUNK
    width = 3 * DK
    heads = held_in.shape[0]
    chips = heads // 2
    count_z, count_x = held_z.shape[0], held_x.shape[0]
    blocks = count_z * count_x

    head = lax.axis_index("head")
    chip, core = head // 2, lax.rem(head, 2)
    me = lax.axis_index("ctx")
    place_x, place_z = me // count_z, lax.rem(me, count_z)
    targets_y = [{"head": lax.rem(chip + offset, chips) * 2 + core} for offset in (1, chips - 1)]
    sibling = {"head": head + 1 - 2 * core}
    targets_z = [
        {"ctx": place_x * count_z + lax.rem(place_z + offset, count_z)} for offset in (1, count_z - 1)
    ]
    targets_x = [
        {"ctx": lax.rem(place_x + offset, count_x) * count_z + place_z} for offset in (1, count_x - 1)
    ]
    after, before = {"ctx": lax.rem(me + 1, blocks)}, {"ctx": lax.rem(me + blocks - 1, blocks)}

    loads = [
        pltpu.make_async_copy(w_proj_ref, w_proj, load_sem.at[0]),
        pltpu.make_async_copy(w_out_ref, w_out, load_sem.at[1]),
    ]
    for load in loads:
        load.start()
    barrier = pltpu.get_barrier_semaphore()
    partners = targets_y + [sibling] + targets_z + targets_x + [after, before]
    for partner in partners:
        pl.semaphore_signal(barrier, inc=1, device_id=partner, device_id_type=MESH)
    pl.semaphore_wait(barrier, len(partners))

    def near(held, number):
        def copy(slot, offset, index, source):
            part = rows // PARTS
            span = pl.ds(index * part, part)
            return pltpu.make_async_remote_copy(
                src_ref=source.at[span],
                dst_ref=held.at[slot, span],
                send_sem=near_send.at[number, offset, index],
                recv_sem=near_recv.at[number, offset, index],
                device_id=sibling,
                device_id_type=MESH,
            )

        return copy

    ring_in = Ring(chip, chips, targets_y, tokens_ref, held_in, send_y.at[0], recv_y.at[0], 2, core, near(held_in, 0))
    ring_out = Ring(chip, chips, targets_y, normed_ref, held_out, send_y.at[1], recv_y.at[1], 2, core, near(held_out, 1))
    ring_z = Ring(place_z, count_z, targets_z, pair_ref, held_z, send_z, recv_z)
    ring_x = Ring(place_x, count_x, targets_x, group_ref, held_x, send_x, recv_x)

    for index in range(PARTS):
        ring_in.begin(index)
    held_in[head] = tokens_ref[...]
    raw_ref[...] = jnp.zeros_like(raw_ref)
    mixing_ref[...] = jnp.zeros_like(mixing_ref)
    out_ref[...] = jnp.zeros_like(out_ref)
    for load in loads:
        load.wait()

    def project(lhs, begin):
        high, low = split(w_proj[pl.ds(begin, 2 * DK), :])
        raw_ref[...] += (
            jnp.dot(lhs[0], high, preferred_element_type=F32)
            + jnp.dot(lhs[0], low, preferred_element_type=F32)
            + jnp.dot(lhs[1], high, preferred_element_type=F32)
        )
        high, low = split(w_mix_ref[:, pl.ds(begin, 2 * DK)])
        dims = (((1,), (1,)), ((), ()))
        mixing_ref[...] += (
            lax.dot_general(lhs[0], high, dims, preferred_element_type=F32)
            + lax.dot_general(lhs[0], low, dims, preferred_element_type=F32)
            + lax.dot_general(lhs[1], high, dims, preferred_element_type=F32)
        )

    multiply_arrivals(ring_in, project)

    rim = pltpu.make_async_remote_copy(
        src_ref=raw_ref.at[pl.ds(rows - RIM, RIM), pl.ds(0, width)],
        dst_ref=prior_ref,
        send_sem=rim_sem.at[0],
        recv_sem=rim_sem.at[1],
        device_id=after,
        device_id_type=MESH,
    )
    padded_ref[RIM:] = raw_ref[:, :width]
    rim.start()

    row_ids = lax.broadcasted_iota(jnp.int32, (CHUNK, CHUNK), 0)
    col_ids = lax.broadcasted_iota(jnp.int32, (CHUNK, CHUNK), 1)
    lower = row_ids >= col_ids
    strict = row_ids > col_ids
    apart = row_ids ^ col_ids
    identity = (row_ids == col_ids).astype(F32)
    ones_lower = lower.astype(BF16)
    ones_upper = (row_ids <= col_ids).astype(BF16)
    rate = rate_ref[0]
    mix = mixing_ref[...]
    weights = softplus(mix)
    mixing_ref[...] = weights
    betas = jax.nn.sigmoid(mix)
    taps = conv_ref[...]

    def prepare(c):
        base = c * CHUNK
        total = jnp.zeros((CHUNK, width), F32)
        for step in range(4):
            first = base + RIM - 3 + step
            total = total + taps[step:step + 1] * padded_ref[first:first + CHUNK]
        total = total * jax.nn.sigmoid(total)
        q, k, v = total[:, :DK], total[:, DK:2 * DK], total[:, 2 * DK:]
        q = q * lax.rsqrt(jnp.sum(q * q, axis=1, keepdims=True) + 1e-06)
        k = k * lax.rsqrt(jnp.sum(k * k, axis=1, keepdims=True) + 1e-06)
        beta = betas[base:base + CHUNK, 0:1]
        drop = jnp.broadcast_to(-rate * weights[base:base + CHUNK, 1:2], (CHUNK, CHUNK))
        high, low = split(drop)
        lowest = (drop - high.astype(F32) - low.astype(F32)).astype(BF16)
        sums = jnp.dot(ones_lower, jnp.concatenate([high, low, lowest], axis=1), preferred_element_type=F32)
        drift = sums[:, :CHUNK] + sums[:, CHUNK:2 * CHUNK] + sums[:, 2 * CHUNK:]
        docs = jnp.broadcast_to(doc_ref[c:c + 1].astype(F32), (CHUNK, CHUNK)).astype(BF16)
        count_t = jnp.dot(docs, ones_upper, preferred_element_type=F32)
        count = count_t.T
        gap = (drift - drift.T) - 20.0 * (count - count_t)
        decay = jnp.where(lower, jnp.exp(jnp.where(lower, gap, 0.0)), 0.0)
        begin = jnp.exp(drift - 20.0 * count)
        last = slice(CHUNK - 1, CHUNK)
        tail = jnp.exp((drift[last] - drift) - 20.0 * (count[last] - count))
        both = product(left(jnp.concatenate([k, q], axis=0)), right(k.T))
        return dict(
            q=q, k=k, gram=jnp.where(strict, beta * both[:CHUNK], 0.0), cross=jnp.where(lower, both[CHUNK:], 0.0),
            decay=decay, begin=begin, end=begin[last], tail=tail, weighted_k=beta * k, weighted_v=beta * v,
        )

    parts = [None] * chunks
    for c in range(1, chunks):
        parts[c] = prepare(c)
    rim.wait_recv()
    padded_ref[:RIM] = jnp.where(me == 0, 0.0, prior_ref[...])
    parts[0] = prepare(0)

    inverses = [identity - jnp.where(apart == 1, part["gram"], 0.0) for part in parts]
    size = 2
    while size < CHUNK:
        member = (apart >= size) & (apart < 2 * size)
        rights = [right(inverse) for inverse in inverses]
        firsts = [product(left(jnp.where(member, part["gram"], 0.0)), rights[c]) for c, part in enumerate(parts)]
        inverses = [inverse - product(left(inverse), right(firsts[c])) for c, inverse in enumerate(inverses)]
        size *= 2

    starts = []
    state = None
    for c, part in enumerate(parts):
        part["x"] = product(left(inverses[c]), right(part["weighted_k"]))
        part["y"] = product(left(part["decay"] * inverses[c]), right(part["weighted_v"]))
        ends_t = jnp.concatenate([part["x"], part["y"] * part["tail"]], axis=1).T
        ended = product(left(ends_t), right(part["k"]))
        pair = jnp.concatenate([part["end"] * (identity - ended[:DK]), ended[DK:]], axis=0)
        starts.append(state)
        state = pair if state is None else join(state, pair)
    pair_ref[...] = state
    held_z[place_z] = state

    def finish(c):
        part = parts[c]
        own = part["begin"] * (part["q"] - product(left(part["cross"]), right(part["x"])))
        near_part = product(left(part["decay"] * part["cross"]), right(part["y"]))
        if starts[c] is not None:
            own_left = left(own)
            near_part = near_part + product(own_left, right(starts[c][DK:].T))
            own = product(own_left, right(starts[c][:DK].T))
        base = c * CHUNK
        carried_ref[base:base + CHUNK] = own
        local_ref[base:base + CHUNK] = mixing_ref[base:base + CHUNK, 2:3] * near_part

    for index in range(PARTS):
        ring_z.begin(index)
    hops = 0
    for c in range(chunks):
        finish(c)
        if c >= 1 and hops < ring_z.half:
            hops += 1
            ring_z.arrive(hops)
    ring_z.run(hops + 1)

    group = reduce_ring(held_z, tree_z, count_z, True)
    group_ref[...] = group
    held_x[place_x] = group
    pair_rows = lax.broadcasted_iota(jnp.int32, (2 * DK, DK), 0)
    pair_cols = lax.broadcasted_iota(jnp.int32, (2 * DK, DK), 1)
    neutral = (pair_rows == pair_cols).astype(F32)
    states, carry = level_states(held_z, tree_z, count_z, place_z, neutral[:DK], neutral)
    for index in range(PARTS):
        ring_x.begin(index)
    done = len(states)

    def mixed(c, states, first):
        base = c * CHUNK
        carried = left(carried_ref[base:base + CHUNK])
        total = local_ref[base:base + CHUNK]
        for number, state in enumerate(states):
            column = first + number
            total = total + mixing_ref[base:base + CHUNK, column:column + 1] * product(carried, state)
        return total

    turned = [right(value.T) for value in states]
    for c in range(chunks):
        local_ref[c * CHUNK:(c + 1) * CHUNK] = mixed(c, turned, 3)
    ring_x.run()
    reduce_ring(held_x, tree_x, count_x, False)
    states, carry = level_states(held_x, tree_x, count_x, place_x, carry, neutral)
    turned = [right(value.T) for value in states]
    for c in range(chunks):
        total = mixed(c, turned, 3 + done)
        scale = lax.rsqrt(jnp.mean(total * total, axis=1, keepdims=True) + 1e-05)
        gate = raw_ref[c * CHUNK:(c + 1) * CHUNK, width:]
        normed = total * scale * gain_ref[...] * (gate * jax.nn.sigmoid(gate))
        normed_ref[c * CHUNK:(c + 1) * CHUNK] = normed
        held_out[head, c * CHUNK:(c + 1) * CHUNK] = normed
        if c >= 1:
            ring_out.begin(c - 1)
    ring_out.begin(chunks - 1)

    def combine(lhs, begin):
        high, low = split(w_out[pl.ds(begin, 2 * DK), :])
        both = jnp.concatenate([high, low], axis=1)
        out = jnp.dot(lhs[0], both, preferred_element_type=F32)
        out_ref[...] += out[:, :DK] + out[:, DK:] + jnp.dot(lhs[1], high, preferred_element_type=F32)

    multiply_arrivals(ring_out, combine)
    rim.wait_send()
    for ring in (ring_in, ring_z, ring_x, ring_out):
        ring.end()


def shards(tokens, w_proj, w_mix, conv_w, rates, doc_start, norm_gain, w_out):
    rows = tokens.shape[0]
    heads = lax.axis_size("head")
    count = lax.axis_size("ctx")
    count_z = min(NZ, count)
    count_x = count // count_z
    vmem = lambda *shape: pltpu.VMEM(shape, F32)
    sems = lambda *shape: pltpu.SemaphoreType.DMA(shape)
    pair = (2 * DK, DK)
    return pl.pallas_call(
        layer,
        out_shape=jax.ShapeDtypeStruct((rows, DK), F32),
        in_specs=[VMEM, ANY, VMEM, VMEM, SMEM, VMEM, VMEM, ANY],
        out_specs=VMEM,
        scratch_shapes=[
            vmem(heads, rows, DK), vmem(heads, rows, DK), vmem(*w_proj.shape), vmem(*w_out.shape),
            vmem(rows, 4 * DK), vmem(rows, w_mix.shape[1]), vmem(rows + RIM, 3 * DK), vmem(RIM, 3 * DK),
            vmem(*pair), vmem(count_z, *pair), vmem(count_z.bit_length() - 2, count_z // 2, *pair),
            vmem(*pair), vmem(count_x, *pair), vmem(max(count_x.bit_length() - 2, 1), count_x // 2, *pair),
            vmem(rows, DK), vmem(rows, DK), vmem(rows, DK),
            sems(2), sems(2), sems(2, 2, heads // 4, PARTS), sems(2, 2, heads // 4, PARTS),
            sems(2, heads // 2, PARTS), sems(2, heads // 2, PARTS),
            sems(2, count_z // 2, PARTS), sems(2, count_z // 2, PARTS),
            sems(2, count_x // 2, PARTS), sems(2, count_x // 2, PARTS),
        ],
        compiler_params=pltpu.CompilerParams(collective_id=0, has_side_effects=True, vmem_limit_bytes=56 << 20),
        name="layer",
    )(tokens, w_proj, w_mix.T, conv_w, rates, doc_start.reshape(-1, CHUNK), norm_gain[None, :], w_out)


def solution(mesh):
    placed = (
        P("ctx", "head"),
        P(None, "head"),
        P(None, "head"),
        P(None, "head"),
        P("head"),
        P("ctx"),
        P("head"),
        P(None, "head"),
    )
    return jax.shard_map(
        shards, mesh=mesh, in_specs=placed, out_specs=P("ctx", "head"), check_vma=False
    )
```

time: 236 us -> 122 us (0.52)
  waiting for transfers between devices: 133 us -> 0 us
  Pallas kernels: 8.68 us -> 119 us
  starting transfers between devices: 56.8 us -> 0 us
  matrix products: 17.9 us -> 0 us
  between operations: 14.5 us -> 0.66 us
    all_gather x2 -> x0, waiting for transfers between devices: 122 us -> none  [the longest x1 67.2 us: shards(): portion = lax.all_gather(tokens, 'head', axis=1, tiled=True)]
    pallas_call x2 -> x1, Pallas kernels: 8.68 us -> 119 us  [shards(): pl.pallas_call(layer, out_shape=jax.ShapeDtypeStruct((rows, DK), F32), in...]
    ppermute x12 -> x0, starting transfers between devices: 56.7 us -> none  [the longest x11 54 us: partner(): return lax.ppermute(value, axis, pairs)]
    dot_general x23 -> x0, matrix products: 17.9 us -> none  [the longest x1 7.34 us: shards(): jnp.dot(portion, w_proj, precision=high, preferred_element_type=F32)]
    ppermute x12 -> x0, waiting for transfers between devices: 10.6 us -> none  [the longest x11 10.6 us: partner(): return lax.ppermute(value, axis, pairs)]
  transfers between devices with their start and end apart: 14 -> 0, of which waited for: 5 -> 0; matrix products, arithmetic and copies ran while one was open for 3% -> 0% of each run, Pallas kernels for 0% -> 0%
where the time goes in v4:
time: 122 us
  Pallas kernels  119 us (98%)
  local copies, waits for them, and re-layouts  1.67 us (1%)
    pallas_call x1, Pallas kernels, shards(): pl.pallas_call(layer, out_shape=jax.ShapeDtypeStruct((rows, DK), F32), in...  119 us

profile of v4, /device:TPU:1, one launch (start us, length us, event | category | flops | bytes accessed | tf_op | source)
XLA Modules:
  0.0 121.6 jit_solution(16959357037198734783)
XLA Ops:
  0.7 119.3 %layer.1 = f32[512,128]{1,0:T(8,128)} custom-call(f32[512,128]{1,0:T(8,128)} %tokens_ref.1, f32[2048,512]{1,0:T(8,128)} %w_proj_ref.1, f32[9,2048]{1,0:T(8,128)} %bitcast.3, f32[4,384]{1,0:T(4,128)} %conv_ref.1, f32[1]{0:T(128)S(6)} %copy.10.rate_ref, s32[4,128]{1,0:T(4,128)} %bitcast.4, f32[1,128]{1,0:T(1,128)} %bitcast.5, f32[2048,128]{1,0:T(8,128)} %w_out_ref.1), custom_call_target="tpu_custom_call" | custom-call | tf_op jit(solution)/shard_map/layer/pallas_call | solution.py:424
  119.9 1.7 %copy.11 = f32[512,128]{1,0:T(8,128)} copy(f32[512,128]{1,0:T(8,128)} %layer.1) | data formatting | bytes 524288

commit v5 on v4

--- a/solution.py
+++ b/solution.py
@@ -11,11 +11,11 @@
 CHUNK = 128
 RIM = 8
 NZ = 16
-PARTS = 4
+PARTS_Y, PARTS_Z, PARTS_X = 4, 8, 4
 MESH = pl.DeviceIdType.MESH
 VMEM = pl.BlockSpec(memory_space=pltpu.VMEM)
 SMEM = pl.BlockSpec(memory_space=pltpu.SMEM)
-ANY = pl.BlockSpec(memory_space=pl.ANY)
+HBM = pl.BlockSpec(memory_space=pltpu.HBM)
 
 
 def split(value):
@@ -49,12 +49,12 @@
 
 
 class Ring:
-    def __init__(self, place, n, targets, source, held, send_sem, recv_sem, stride=1, phase=0, pass_on=None):
+    def __init__(self, parts, place, n, targets, source, held, send_sem, recv_sem, stride=1, phase=0, pass_on=None):
         self.place, self.n, self.targets, self.source, self.held = place, n, targets, source, held
         self.send_sem, self.recv_sem, self.stride, self.phase = send_sem, recv_sem, stride, phase
-        self.pass_on = pass_on
+        self.pass_on, self.parts = pass_on, parts
         self.half = n // 2
-        self.part = source.shape[0] // PARTS
+        self.part = source.shape[0] // parts
 
     def slot(self, place):
         return place * self.stride + self.phase
@@ -63,7 +63,7 @@
         return pl.ds(index * self.part, self.part)
 
     def goes(self, direction, hop, index):
-        longest = self.half if (index < PARTS // 2) == (direction == 0) else self.half - 1
+        longest = self.half if (index < self.parts // 2) == (direction == 0) else self.half - 1
         return hop <= longest
 
     def offset(self, direction, hop):
@@ -89,7 +89,7 @@
             self.pass_on(self.slot(self.place), 0, index, self.source).start()
 
     def arrive(self, hop, guard=True):
-        for index in range(PARTS):
+        for index in range(self.parts):
             for direction in range(2):
                 here = guard & self.goes(direction, hop, index)
 
@@ -116,7 +116,7 @@
         lax.fori_loop(first, self.half + 1, step, 0)
 
     def end(self):
-        for index in range(PARTS):
+        for index in range(self.parts):
             for direction in range(2):
                 for hop in range(self.half):
                     if self.goes(direction, hop + 1, index):
@@ -126,6 +126,63 @@
                     self.pass_on(self.slot(self.place), offset, index, self.source).wait_send()
 
 
+class PairRing:
+    def __init__(self, parts, place, n, targets, source, held, send_sem, recv_sem):
+        self.place, self.n, self.targets, self.source, self.held = place, n, targets, source, held
+        self.send_sem, self.recv_sem, self.parts = send_sem, recv_sem, parts
+        self.last = n // 2 - 1
+        self.part = source.shape[0] // parts
+
+    def copy(self, hop, index):
+        rightward = lax.rem(self.place + hop, 2) == 1
+        origin = lax.rem(self.place + jnp.where(rightward, self.n - hop, hop), self.n)
+        slot = origin // 2
+        direction = jnp.where(rightward, 0, 1)
+        span = pl.ds(index * self.part, self.part)
+        source = self.source if isinstance(hop, int) and hop == 0 else self.held.at[slot]
+        return pltpu.make_async_remote_copy(
+            src_ref=source.at[span],
+            dst_ref=self.held.at[slot, span],
+            send_sem=self.send_sem.at[direction, hop, index],
+            recv_sem=self.recv_sem.at[direction, hop, index],
+            device_id={"ctx": jnp.where(rightward, self.targets[0]["ctx"], self.targets[1]["ctx"])},
+            device_id_type=MESH,
+        )
+
+    def begin(self):
+        for index in range(self.parts):
+            self.copy(0, index).start()
+
+    def run(self):
+        def step(hop, carry):
+            for index in range(self.parts):
+                origin = lax.rem(self.place + jnp.where(lax.rem(self.place + hop, 2) == 1, self.n - hop, hop), self.n)
+                direction = jnp.where(lax.rem(self.place + hop, 2) == 1, 0, 1)
+                span = pl.ds(index * self.part, self.part)
+                slot = self.held.at[origin // 2, span]
+                pltpu.make_async_remote_copy(
+                    src_ref=slot,
+                    dst_ref=slot,
+                    send_sem=self.send_sem.at[direction, hop - 1, index],
+                    recv_sem=self.recv_sem.at[direction, hop - 1, index],
+                    device_id=self.targets[0],
+                    device_id_type=MESH,
+                ).wait_recv()
+
+                @pl.when(hop < self.last)
+                def _():
+                    self.copy(hop, index).start()
+
+            return carry
+
+        lax.fori_loop(1, self.last + 1, step, 0)
+
+    def end(self):
+        for index in range(self.parts):
+            for hop in range(self.last):
+                self.copy(hop, index).wait_send()
+
+
 def multiply_arrivals(ring, multiply):
     def step(hop, carry):
         ring.arrive(hop, hop >= 1)
@@ -133,7 +190,7 @@
         def block(which, inner):
             offset = lax.rem(jnp.where(which == 0, hop, ring.n - hop), ring.n)
             there = lax.rem(ring.place + offset, ring.n)
-            for index in range(PARTS):
+            for index in range(ring.parts):
                 other = there * 2 + 1 - ring.phase
                 ring.pass_on(other, offset, index, ring.held.at[other]).wait_recv()
             lhs = jnp.concatenate([ring.held[there * 2], ring.held[there * 2 + 1]], axis=1)
@@ -170,17 +227,17 @@
     return states, carry
 
 
-def layer(tokens_ref, w_proj_ref, w_mix_ref, conv_ref, rate_ref, doc_ref, gain_ref, w_out_ref, out_ref,
-          held_in, held_out, w_proj, w_out, raw_ref, mixing_ref, padded_ref, prior_ref,
-          pair_ref, held_z, tree_z, group_ref, held_x, tree_x, local_ref, carried_ref, normed_ref,
-          load_sem, rim_sem, send_y, recv_y, near_send, near_recv,
+def layer(tokens_ref, w_proj_ref, w_mix_hbm, conv_hbm, rate_ref, doc_hbm, gain_hbm, w_out_ref, out_ref,
+          held_in, held_out, w_proj, w_out, w_mix_ref, conv_ref, doc_ref, gain_ref, raw_ref, mixing_ref, padded_ref, prior_ref,
+          pair_ref, buddy_ref, near_pair_ref, held_z, tree_z, group_ref, held_x, tree_x, local_ref, carried_ref, normed_ref, kept_ref, start_ref,
+          load_sem, rim_sem, buddy_sem, send_y, recv_y, near_send, near_recv,
           send_z, recv_z, send_x, recv_x):
     rows = tokens_ref.shape[0]
     chunks = rows // CHUNK
     width = 3 * DK
     heads = held_in.shape[0]
     chips = heads // 2
-    count_z, count_x = held_z.shape[0], held_x.shape[0]
+    count_z, count_x = 2 * held_z.shape[0], held_x.shape[0]
     blocks = count_z * count_x
 
     head = lax.axis_index("head")
@@ -197,10 +254,12 @@
     ]
     after, before = {"ctx": lax.rem(me + 1, blocks)}, {"ctx": lax.rem(me + blocks - 1, blocks)}
 
-    loads = [
-        pltpu.make_async_copy(w_proj_ref, w_proj, load_sem.at[0]),
-        pltpu.make_async_copy(w_out_ref, w_out, load_sem.at[1]),
-    ]
+    first_load = pltpu.make_async_copy(tokens_ref, held_in.at[head], load_sem.at[0])
+    first_load.start()
+    pairs = [(w_mix_hbm, w_mix_ref), (w_proj_ref, w_proj), (conv_hbm, conv_ref), (doc_hbm, doc_ref),
+             (gain_hbm, gain_ref), (w_out_ref, w_out)]
+    loads = [pltpu.make_async_copy(source, target, load_sem.at[1 + index])
+             for index, (source, target) in enumerate(pairs)]
     for load in loads:
         load.start()
     barrier = pltpu.get_barrier_semaphore()
@@ -211,7 +270,7 @@
 
     def near(held, number):
         def copy(slot, offset, index, source):
-            part = rows // PARTS
+            part = rows // PARTS_Y
             span = pl.ds(index * part, part)
             return pltpu.make_async_remote_copy(
                 src_ref=source.at[span],
@@ -224,14 +283,23 @@
 
         return copy
 
-    ring_in = Ring(chip, chips, targets_y, tokens_ref, held_in, send_y.at[0], recv_y.at[0], 2, core, near(held_in, 0))
-    ring_out = Ring(chip, chips, targets_y, normed_ref, held_out, send_y.at[1], recv_y.at[1], 2, core, near(held_out, 1))
-    ring_z = Ring(place_z, count_z, targets_z, pair_ref, held_z, send_z, recv_z)
-    ring_x = Ring(place_x, count_x, targets_x, group_ref, held_x, send_x, recv_x)
-
-    for index in range(PARTS):
+    ring_in = Ring(PARTS_Y, chip, chips, targets_y, held_in.at[head], held_in, send_y.at[0], recv_y.at[0], 2, core, near(held_in, 0))
+    ring_out = Ring(PARTS_Y, chip, chips, targets_y, normed_ref, held_out, send_y.at[1], recv_y.at[1], 2, core, near(held_out, 1))
+    ring_z = PairRing(PARTS_Z, place_z, count_z, targets_z, near_pair_ref, held_z, send_z, recv_z)
+    odd = lax.rem(place_z, 2) == 1
+    buddy = pltpu.make_async_remote_copy(
+        src_ref=pair_ref,
+        dst_ref=buddy_ref,
+        send_sem=buddy_sem.at[0],
+        recv_sem=buddy_sem.at[1],
+        device_id={"ctx": me + jnp.where(odd, -1, 1)},
+        device_id_type=MESH,
+    )
+    ring_x = Ring(PARTS_X, place_x, count_x, targets_x, group_ref, held_x, send_x, recv_x)
+
+    first_load.wait()
+    for index in range(PARTS_Y):
         ring_in.begin(index)
-    held_in[head] = tokens_ref[...]
     raw_ref[...] = jnp.zeros_like(raw_ref)
     mixing_ref[...] = jnp.zeros_like(mixing_ref)
     out_ref[...] = jnp.zeros_like(out_ref)
@@ -279,18 +347,23 @@
     weights = softplus(mix)
     mixing_ref[...] = weights
     betas = jax.nn.sigmoid(mix)
-    taps = conv_ref[...]
+
+    def convolve(base, first_column, columns):
+        total = jnp.zeros((CHUNK, columns), F32)
+        span = pl.ds(first_column, columns)
+        window = padded_ref[pl.ds(base, CHUNK + RIM), span]
+        for step in range(4):
+            first = RIM - 3 + step
+            total = total + conv_ref[step:step + 1, span] * window[first:first + CHUNK]
+        return total * jax.nn.sigmoid(total)
+
+    def unit(value):
+        return value * lax.rsqrt(jnp.sum(value * value, axis=1, keepdims=True) + 1e-06)
 
     def prepare(c):
         base = c * CHUNK
-        total = jnp.zeros((CHUNK, width), F32)
-        for step in range(4):
-            first = base + RIM - 3 + step
-            total = total + taps[step:step + 1] * padded_ref[first:first + CHUNK]
-        total = total * jax.nn.sigmoid(total)
-        q, k, v = total[:, :DK], total[:, DK:2 * DK], total[:, 2 * DK:]
-        q = q * lax.rsqrt(jnp.sum(q * q, axis=1, keepdims=True) + 1e-06)
-        k = k * lax.rsqrt(jnp.sum(k * k, axis=1, keepdims=True) + 1e-06)
+        both = convolve(base, DK, 2 * DK)
+        k, v = unit(both[:, :DK]), both[:, DK:]
         beta = betas[base:base + CHUNK, 0:1]
         drop = jnp.broadcast_to(-rate * weights[base:base + CHUNK, 1:2], (CHUNK, CHUNK))
         high, low = split(drop)
@@ -305,11 +378,11 @@
         begin = jnp.exp(drift - 20.0 * count)
         last = slice(CHUNK - 1, CHUNK)
         tail = jnp.exp((drift[last] - drift) - 20.0 * (count[last] - count))
-        both = product(left(jnp.concatenate([k, q], axis=0)), right(k.T))
-        return dict(
-            q=q, k=k, gram=jnp.where(strict, beta * both[:CHUNK], 0.0), cross=jnp.where(lower, both[CHUNK:], 0.0),
-            decay=decay, begin=begin, end=begin[last], tail=tail, weighted_k=beta * k, weighted_v=beta * v,
-        )
+        gram = jnp.where(strict, beta * product(left(k), right(k.T)), 0.0)
+        kept_ref[c, 0] = k
+        kept_ref[c, 1] = decay
+        kept_ref[c, 2] = begin
+        return dict(k=k, gram=gram, decay=decay, end=begin[last], tail=tail, weighted_k=beta * k, weighted_v=beta * v)
 
     parts = [None] * chunks
     for c in range(1, chunks):
@@ -327,50 +400,59 @@
         inverses = [inverse - product(left(inverse), right(firsts[c])) for c, inverse in enumerate(inverses)]
         size *= 2
 
-    starts = []
-    state = None
-    for c, part in enumerate(parts):
-        part["x"] = product(left(inverses[c]), right(part["weighted_k"]))
-        part["y"] = product(left(part["decay"] * inverses[c]), right(part["weighted_v"]))
-        ends_t = jnp.concatenate([part["x"], part["y"] * part["tail"]], axis=1).T
-        ended = product(left(ends_t), right(part["k"]))
-        pair = jnp.concatenate([part["end"] * (identity - ended[:DK]), ended[DK:]], axis=0)
-        starts.append(state)
-        state = pair if state is None else join(state, pair)
-    pair_ref[...] = state
-    held_z[place_z] = state
-
-    def finish(c):
-        part = parts[c]
-        own = part["begin"] * (part["q"] - product(left(part["cross"]), right(part["x"])))
-        near_part = product(left(part["decay"] * part["cross"]), right(part["y"]))
-        if starts[c] is not None:
-            own_left = left(own)
-            near_part = near_part + product(own_left, right(starts[c][DK:].T))
-            own = product(own_left, right(starts[c][:DK].T))
-        base = c * CHUNK
-        carried_ref[base:base + CHUNK] = own
-        local_ref[base:base + CHUNK] = mixing_ref[base:base + CHUNK, 2:3] * near_part
-
-    for index in range(PARTS):
-        ring_z.begin(index)
-    hops = 0
-    for c in range(chunks):
-        finish(c)
-        if c >= 1 and hops < ring_z.half:
-            hops += 1
-            ring_z.arrive(hops)
-    ring_z.run(hops + 1)
-
-    group = reduce_ring(held_z, tree_z, count_z, True)
-    group_ref[...] = group
-    held_x[place_x] = group
     pair_rows = lax.broadcasted_iota(jnp.int32, (2 * DK, DK), 0)
     pair_cols = lax.broadcasted_iota(jnp.int32, (2 * DK, DK), 1)
     neutral = (pair_rows == pair_cols).astype(F32)
-    states, carry = level_states(held_z, tree_z, count_z, place_z, neutral[:DK], neutral)
-    for index in range(PARTS):
+    state = None
+    for c, part in enumerate(parts):
+        factor_x = product(left(inverses[c]), right(part["weighted_k"]))
+        factor_y = product(left(part["decay"] * inverses[c]), right(part["weighted_v"]))
+        kept_ref[c, 3] = factor_x
+        kept_ref[c, 4] = factor_y
+        ends_t = jnp.concatenate([factor_x, factor_y * part["tail"]], axis=1).T
+        ended = product(left(ends_t), right(part["k"]))
+        pair = jnp.concatenate([part["end"] * (identity - ended[:DK]), ended[DK:]], axis=0)
+        start_ref[c] = neutral if state is None else state
+        state = pair if state is None else join(state, pair)
+    pair_ref[...] = state
+    held_z[place_z // 2] = state
+    buddy.start()
+
+    def finish(c):
+        base = pl.multiple_of(c * CHUNK, CHUNK)
+        q = unit(convolve(base, 0, DK))
+        k, decay, begin, factor_x, factor_y = [kept_ref[c, index] for index in range(5)]
+        cross = jnp.where(lower, product(left(q), right(k.T)), 0.0)
+        own = left(begin * (q - product(left(cross), right(factor_x))))
+        near_part = product(left(decay * cross), right(factor_y))
+        near_part = near_part + product(own, right(start_ref[c, DK:].T))
+        span = pl.ds(base, CHUNK)
+        carried_ref[span] = product(own, right(start_ref[c, :DK].T))
+        local_ref[span] = mixing_ref[span, 2:3] * near_part
+
+    def finish_step(c, carry):
+        finish(c)
+        return carry
+
+    early = chunks - 1
+    lax.fori_loop(0, early, finish_step, 0)
+    buddy.wait_recv()
+    mine, other = pair_ref[...], buddy_ref[...]
+    near_pair = join(jnp.where(odd, other, mine), jnp.where(odd, mine, other))
+    near_pair_ref[...] = near_pair
+    held_z[place_z // 2] = near_pair
+    ring_z.begin()
+    lax.fori_loop(early, chunks, finish_step, 0)
+    ring_z.run()
+
+    group = reduce_ring(held_z, tree_z, count_z // 2, True)
+    group_ref[...] = group
+    held_x[place_x] = group
+    for index in range(PARTS_X):
         ring_x.begin(index)
+    nearest = jnp.where(odd, buddy_ref[...], neutral)
+    states, carry = level_states(held_z, tree_z, count_z // 2, place_z // 2, nearest[:DK], neutral)
+    states = [nearest[DK:]] + states
     done = len(states)
 
     def mixed(c, states, first):
@@ -389,6 +471,11 @@
     reduce_ring(held_x, tree_x, count_x, False)
     states, carry = level_states(held_x, tree_x, count_x, place_x, carry, neutral)
     turned = [right(value.T) for value in states]
+
+    def send(c):
+        for index in range(c * PARTS_Y // chunks, (c + 1) * PARTS_Y // chunks):
+            ring_out.begin(index)
+
     for c in range(chunks):
         total = mixed(c, turned, 3 + done)
         scale = lax.rsqrt(jnp.mean(total * total, axis=1, keepdims=True) + 1e-05)
@@ -397,8 +484,8 @@
         normed_ref[c * CHUNK:(c + 1) * CHUNK] = normed
         held_out[head, c * CHUNK:(c + 1) * CHUNK] = normed
         if c >= 1:
-            ring_out.begin(c - 1)
-    ring_out.begin(chunks - 1)
+            send(c - 1)
+    send(chunks - 1)
 
     def combine(lhs, begin):
         high, low = split(w_out[pl.ds(begin, 2 * DK), :])
@@ -408,6 +495,7 @@
 
     multiply_arrivals(ring_out, combine)
     rim.wait_send()
+    buddy.wait_send()
     for ring in (ring_in, ring_z, ring_x, ring_out):
         ring.end()
 
@@ -424,18 +512,21 @@
     return pl.pallas_call(
         layer,
         out_shape=jax.ShapeDtypeStruct((rows, DK), F32),
-        in_specs=[VMEM, ANY, VMEM, VMEM, SMEM, VMEM, VMEM, ANY],
+        in_specs=[HBM, HBM, HBM, HBM, SMEM, HBM, HBM, HBM],
         out_specs=VMEM,
         scratch_shapes=[
             vmem(heads, rows, DK), vmem(heads, rows, DK), vmem(*w_proj.shape), vmem(*w_out.shape),
+            vmem(w_mix.shape[1], w_mix.shape[0]), vmem(*conv_w.shape),
+            pltpu.VMEM((rows // CHUNK, CHUNK), jnp.int32), vmem(1, DK),
             vmem(rows, 4 * DK), vmem(rows, w_mix.shape[1]), vmem(rows + RIM, 3 * DK), vmem(RIM, 3 * DK),
-            vmem(*pair), vmem(count_z, *pair), vmem(count_z.bit_length() - 2, count_z // 2, *pair),
+            vmem(*pair), vmem(*pair), vmem(*pair), vmem(count_z // 2, *pair),
+            vmem(max(count_z.bit_length() - 3, 1), max(count_z // 4, 1), *pair),
             vmem(*pair), vmem(count_x, *pair), vmem(max(count_x.bit_length() - 2, 1), count_x // 2, *pair),
-            vmem(rows, DK), vmem(rows, DK), vmem(rows, DK),
-            sems(2), sems(2), sems(2, 2, heads // 4, PARTS), sems(2, 2, heads // 4, PARTS),
-            sems(2, heads // 2, PARTS), sems(2, heads // 2, PARTS),
-            sems(2, count_z // 2, PARTS), sems(2, count_z // 2, PARTS),
-            sems(2, count_x // 2, PARTS), sems(2, count_x // 2, PARTS),
+            vmem(rows, DK), vmem(rows, DK), vmem(rows, DK), vmem(rows // CHUNK, 5, CHUNK, CHUNK), vmem(rows // CHUNK, *pair),
+            sems(7), sems(2), sems(2), sems(2, 2, heads // 4, PARTS_Y), sems(2, 2, heads // 4, PARTS_Y),
+            sems(2, heads // 2, PARTS_Y), sems(2, heads // 2, PARTS_Y),
+            sems(2, count_z // 2, PARTS_Z), sems(2, count_z // 2, PARTS_Z),
+            sems(2, count_x // 2, PARTS_X), sems(2, count_x // 2, PARTS_X),
         ],
         compiler_params=pltpu.CompilerParams(collective_id=0, has_side_effects=True, vmem_limit_bytes=56 << 20),
         name="layer",

time: 122 us -> 120 us (0.984)
  Pallas kernels: 119 us -> 117 us
    pallas_call x1, Pallas kernels: 119 us -> 117 us  [shards(): pl.pallas_call(layer, out_shape=jax.ShapeDtypeStruct((rows, DK), F32), in...]
where the time goes in v5:
time: 120 us
  Pallas kernels  117 us (98%)
  local copies, waits for them, and re-layouts  1.67 us (1%)
    pallas_call x1, Pallas kernels, shards(): pl.pallas_call(layer, out_shape=jax.ShapeDtypeStruct((rows, DK), F32), in...  117 us

profile of v5, /device:TPU:1, one launch (start us, length us, event | category | flops | bytes accessed | tf_op | source)
XLA Modules:
  0.0 119.6 jit_solution(10384884521305127047)
XLA Ops:
  0.7 117.2 %layer.1 = f32[512,128]{1,0:T(8,128)} custom-call(f32[512,128]{1,0:T(8,128)} %tokens_ref.1, f32[2048,512]{1,0:T(8,128)} %w_proj_ref.1, f32[9,2048]{1,0:T(8,128)} %bitcast.3, f32[4,384]{1,0:T(4,128)} %conv_hbm.1, f32[1]{0:T(128)S(6)} %copy.10.rate_ref, s32[4,128]{1,0:T(4,128)} %bitcast.4, f32[1,128]{1,0:T(1,128)} %bitcast.5, f32[2048,128]{1,0:T(8,128)} %w_out_ref.1), custom_call_target="tpu_custom_call" | custom-call | tf_op jit(solution)/shard_map/layer/pallas_call | solution.py:512
  117.9 1.7 %copy.11 = f32[512,128]{1,0:T(8,128)} copy(f32[512,128]{1,0:T(8,128)} %layer.1) | data formatting | bytes 524288

commit v6 on v5

--- a/solution.py
+++ b/solution.py
@@ -11,7 +11,7 @@
 CHUNK = 128
 RIM = 8
 NZ = 16
-PARTS_Y, PARTS_Z, PARTS_X = 4, 8, 4
+PARTS_Y, PARTS_Z, PARTS_X = 4, 4, 4
 MESH = pl.DeviceIdType.MESH
 VMEM = pl.BlockSpec(memory_space=pltpu.VMEM)
 SMEM = pl.BlockSpec(memory_space=pltpu.SMEM)

time: 120 us -> 119 us (level)
  no operation moved by 1% of the time
where the time goes in v6:
time: 119 us
  Pallas kernels  116 us (97%)
  local copies, waits for them, and re-layouts  1.67 us (1%)
    pallas_call x1, Pallas kernels, shards(): pl.pallas_call(layer, out_shape=jax.ShapeDtypeStruct((rows, DK), F32), in...  116 us

profile of v6, /device:TPU:1, one launch (start us, length us, event | category | flops | bytes accessed | tf_op | source)
XLA Modules:
  0.0 118.7 jit_solution(11544819025384854708)
XLA Ops:
  0.7 116.3 %layer.1 = f32[512,128]{1,0:T(8,128)} custom-call(f32[512,128]{1,0:T(8,128)} %tokens_ref.1, f32[2048,512]{1,0:T(8,128)} %w_proj_ref.1, f32[9,2048]{1,0:T(8,128)} %bitcast.3, f32[4,384]{1,0:T(4,128)} %conv_hbm.1, f32[1]{0:T(128)S(6)} %copy.10.rate_ref, s32[4,128]{1,0:T(4,128)} %bitcast.4, f32[1,128]{1,0:T(1,128)} %bitcast.5, f32[2048,128]{1,0:T(8,128)} %w_out_ref.1), custom_call_target="tpu_custom_call" | custom-call | tf_op jit(solution)/shard_map/layer/pallas_call | solution.py:512
  117.0 1.7 %copy.11 = f32[512,128]{1,0:T(8,128)} copy(f32[512,128]{1,0:T(8,128)} %layer.1) | data formatting | bytes 524288
